TPU v7x, 256 devices: a whole 4x4x8 slice. The times are simulated.
256 devices in a mesh: blk: 256 (over x, y, z, core).
Axes of the slice: x: 4, y: 4, z: 8, core: 2. Of those that a mesh axis runs over, the one named last changes fastest.
Arguments:
- right_side: float32 [32768, 128], P('blk')
- kernel_tiles: float32 [256, 129, 128, 128], P('blk'), as said below
- route_pairs: int32 [129, 2], replicated, may hold values from 0 to 30
Outputs:
- solution: float32 [32768, 128], P('blk')
- residual: float32 [32768, 128], P('blk')
Inputs may be any that keep to these rules, and one draw needn't show every extreme that they name: kernel_tiles makes K symmetric with a positive diagonal of about 1 to 16 inside the diagonal tiles; K is positive definite.
All inputs are finite; a program needn't handle non-finite values.
Results may differ from a plain program's by a relative error of at most 0.0003.
Values sent between devices are 32-bit elements; how exact they have to be, the bound alone decides.
A program may use at most 128 MiB of HBM per device.

v0:
```python
import jax
import jax.numpy as jnp
from jax import lax
from jax.sharding import PartitionSpec as P


def shifted(value, axis, steps):
    count = lax.axis_size(axis)
    pairs = [(source, (source + steps) % count) for source in range(count)]
    return lax.ppermute(value, axis, pairs)


def collect_cover(vector, cover_list):
    pieces = [vector[None]]
    for offset in cover_list[1:]:
        pieces.append(shifted(vector, "blk", -offset)[None])
    return jnp.concatenate(pieces, axis=0)


def fold_partials(partial_value, cover_list):
    summed = partial_value[0]
    for place, offset in enumerate(cover_list[1:]):
        summed = summed + shifted(partial_value[place + 1], "blk", offset)
    return summed


def column_total(values):
    return lax.psum(jnp.sum(values, axis=0), "blk")


def per_device(right_side, kernel_tiles, route_pairs):
    blocks_total = lax.axis_size("blk")
    window_len = max(8, min(16, blocks_total // 8))
    cover_list = [k for k in range(window_len)] + [
        k * window_len for k in range(1, blocks_total // window_len)
    ]
    cover_len = len(cover_list)
    own_tiles = kernel_tiles[0]
    slot_total = own_tiles.shape[0]
    cover_ids = jnp.arange(cover_len, dtype=jnp.int32)
    slot_ids = jnp.arange(slot_total, dtype=jnp.int32)
    mirror = ((slot_ids > 0) & (slot_ids < slot_total - 1)).astype(jnp.float32)
    row_hot = (route_pairs[:, 0:1] == cover_ids[None, :]).astype(jnp.float32)
    col_hot = (route_pairs[:, 1:2] == cover_ids[None, :]).astype(jnp.float32) * mirror[:, None]
    residual = right_side
    norm_now = column_total(residual * residual)
    blocks = collect_cover(right_side, cover_list)
    by_row = jnp.einsum(
        "tij,tjr->tir",
        own_tiles,
        jnp.take(blocks, route_pairs[:, 1], axis=0),
        precision=lax.Precision.HIGHEST,
    )
    by_col = jnp.einsum(
        "tji,tjr->tir",
        own_tiles,
        jnp.take(blocks, route_pairs[:, 0], axis=0),
        precision=lax.Precision.HIGHEST,
    )
    partial_value = jnp.einsum("tc,tbr->cbr", row_hot, by_row, precision=lax.Precision.HIGHEST)
    partial_value = partial_value + jnp.einsum(
        "tc,tbr->cbr", col_hot, by_col, precision=lax.Precision.HIGHEST
    )
    image = fold_partials(partial_value, cover_list)
    step_len = norm_now / column_total(right_side * image)
    solution = step_len * right_side
    residual = residual - step_len * image
    return (solution, residual)


def solution(mesh):
    return jax.shard_map(
        per_device,
        mesh=mesh,
        in_specs=(P("blk", None), P("blk", None, None, None), P()),
        out_specs=(P("blk", None), P("blk", None)),
        check_vma=False,
    )
```

profile of v0, /device:TPU:1, one launch (start us, length us, event | category | flops | bytes accessed | tf_op | source)
XLA Modules:
  0.0 538.1 jit_solution(14289325914824898295)
XLA Ops:
  8.7 12.8 %collective-permute-start = (f32[128,128]{1,0:T(8,128)}, f32[128,128]{1,0:T(8,128)S(1)}, u32[]{:S(2)}, u32[]{:S(2)}) collective-permute-start(f32[128,128]{1,0:T(8,128)} %param.5), channel_id=1, source_target_pairs={{0,255},{1,0},{2,1},{3,2},{4,3},{5,4},{6,5},{7,6},{8,7},{9,8},{10,... | collective-permute-start | bytes 196616 | tf_op jit(solution)/shard_map/ppermute | solution.py:10
  25.4 10.6 %collective-permute-start.1 = (f32[128,128]{1,0:T(8,128)}, f32[128,128]{1,0:T(8,128)S(1)}, u32[]{:S(2)}, u32[]{:S(2)}) collective-permute-start(f32[128,128]{1,0:T(8,128)} %param.5), channel_id=1, source_target_pairs={{0,254},{1,255},{2,0},{3,1},{4,2},{5,3},{6,4},{7,5},{8,6},{9,7},{1... | collective-permute-start | bytes 196616 | tf_op jit(solution)/shard_map/ppermute | solution.py:10
  39.8 11.5 %collective-permute-start.2 = (f32[128,128]{1,0:T(8,128)}, f32[128,128]{1,0:T(8,128)S(1)}, u32[]{:S(2)}, u32[]{:S(2)}) collective-permute-start(f32[128,128]{1,0:T(8,128)} %param.5), channel_id=1, source_target_pairs={{0,253},{1,254},{2,255},{3,0},{4,1},{5,2},{6,3},{7,4},{8,5},{9,6},... | collective-permute-start | bytes 196616 | tf_op jit(solution)/shard_map/ppermute | solution.py:10
  56.5 10.4 %collective-permute-start.3 = (f32[128,128]{1,0:T(8,128)}, f32[128,128]{1,0:T(8,128)S(1)}, u32[]{:S(2)}, u32[]{:S(2)}) collective-permute-start(f32[128,128]{1,0:T(8,128)} %param.5), channel_id=1, source_target_pairs={{0,252},{1,253},{2,254},{3,255},{4,0},{5,1},{6,2},{7,3},{8,4},{9,5... | collective-permute-start | bytes 196616 | tf_op jit(solution)/shard_map/ppermute | solution.py:10
  71.9 12.0 %collective-permute-start.4 = (f32[128,128]{1,0:T(8,128)}, f32[128,128]{1,0:T(8,128)S(1)}, u32[]{:S(2)}, u32[]{:S(2)}) collective-permute-start(f32[128,128]{1,0:T(8,128)} %param.5), channel_id=1, source_target_pairs={{0,251},{1,252},{2,253},{3,254},{4,255},{5,0},{6,1},{7,2},{8,3},{9... | collective-permute-start | bytes 196616 | tf_op jit(solution)/shard_map/ppermute | solution.py:10
  90.4 10.3 %collective-permute-start.5 = (f32[128,128]{1,0:T(8,128)}, f32[128,128]{1,0:T(8,128)S(1)}, u32[]{:S(2)}, u32[]{:S(2)}) collective-permute-start(f32[128,128]{1,0:T(8,128)} %param.5), channel_id=1, source_target_pairs={{0,250},{1,251},{2,252},{3,253},{4,254},{5,255},{6,0},{7,1},{8,2},... | collective-permute-start | bytes 196616 | tf_op jit(solution)/shard_map/ppermute | solution.py:10
  106.8 12.0 %collective-permute-start.6 = (f32[128,128]{1,0:T(8,128)}, f32[128,128]{1,0:T(8,128)S(1)}, u32[]{:S(2)}, u32[]{:S(2)}) collective-permute-start(f32[128,128]{1,0:T(8,128)} %param.5), channel_id=1, source_target_pairs={{0,249},{1,250},{2,251},{3,252},{4,253},{5,254},{6,255},{7,0},{8,1... | collective-permute-start | bytes 196616 | tf_op jit(solution)/shard_map/ppermute | solution.py:10
  118.7 8.8 %collective-permute-done.6 = f32[128,128]{1,0:T(8,128)S(1)} collective-permute-done((f32[128,128]{1,0:T(8,128)}, f32[128,128]{1,0:T(8,128)S(1)}, u32[]{:S(2)}, u32[]{:S(2)}) %collective-permute-start.6) | collective-permute-done | bytes 65568 | tf_op jit(solution)/shard_map/ppermute | solution.py:10
  127.5 8.2 %collective-permute-start.7 = (f32[128,128]{1,0:T(8,128)}, f32[128,128]{1,0:T(8,128)S(1)}, u32[]{:S(2)}, u32[]{:S(2)}) collective-permute-start(f32[128,128]{1,0:T(8,128)} %param.5), channel_id=1, source_target_pairs={{0,248},{1,249},{2,250},{3,251},{4,252},{5,253},{6,254},{7,255},{8... | collective-permute-start | bytes 196616 | tf_op jit(solution)/shard_map/ppermute | solution.py:10
  135.7 10.0 %collective-permute-done.7 = f32[128,128]{1,0:T(8,128)S(1)} collective-permute-done((f32[128,128]{1,0:T(8,128)}, f32[128,128]{1,0:T(8,128)S(1)}, u32[]{:S(2)}, u32[]{:S(2)}) %collective-permute-start.7) | collective-permute-done | bytes 65568 | tf_op jit(solution)/shard_map/ppermute | solution.py:10
  152.4 10.1 %collective-permute-done.8 = f32[128,128]{1,0:T(8,128)S(1)} collective-permute-done((f32[128,128]{1,0:T(8,128)}, f32[128,128]{1,0:T(8,128)S(1)}, u32[]{:S(2)}, u32[]{:S(2)}) %collective-permute-start.8) | collective-permute-done | bytes 65568 | tf_op jit(solution)/shard_map/ppermute | solution.py:10
  169.5 9.7 %collective-permute-done.9 = f32[128,128]{1,0:T(8,128)S(1)} collective-permute-done((f32[128,128]{1,0:T(8,128)}, f32[128,128]{1,0:T(8,128)S(1)}, u32[]{:S(2)}, u32[]{:S(2)}) %collective-permute-start.9) | collective-permute-done | bytes 65568 | tf_op jit(solution)/shard_map/ppermute | solution.py:10
  185.4 8.9 %collective-permute-start.11 = (f32[128,128]{1,0:T(8,128)}, f32[128,128]{1,0:T(8,128)S(1)}, u32[]{:S(2)}, u32[]{:S(2)}) collective-permute-start(f32[128,128]{1,0:T(8,128)} %param.5), channel_id=1, source_target_pairs={{0,244},{1,245},{2,246},{3,247},{4,248},{5,249},{6,250},{7,251},{8... | collective-permute-start | bytes 196616 | tf_op jit(solution)/shard_map/ppermute | solution.py:10
  208.4 9.2 %collective-permute-start.14 = (f32[128,128]{1,0:T(8,128)}, f32[128,128]{1,0:T(8,128)S(1)}, u32[]{:S(2)}, u32[]{:S(2)}) collective-permute-start(f32[128,128]{1,0:T(8,128)} %param.5), channel_id=1, source_target_pairs={{0,241},{1,242},{2,243},{3,244},{4,245},{5,246},{6,247},{7,248},{8... | collective-permute-start | bytes 196616 | tf_op jit(solution)/shard_map/ppermute | solution.py:10
  287.8 19.8 %fusion.4 = f32[129,128,128]{2,1,0:T(8,128)} fusion(f32[1,129,128,128]{3,2,1,0:T(8,128)} %param.6, f32[129,128,128]{2,1,0:T(8,128)} %gather_fusion.1, pred[129]{0:T(512)(128)(4,1)S(1)} %compare_and_fusion), kind=kOutput, calls=%fused_computation.6 | convolution fusion | flops 3248504832 | bytes 25362560 | tf_op jit(solution)/shard_map/tji,tjr->tir/dot_general | solution.py:54
  307.6 9.5 %copy.38 = f32[129,128,128]{1,0,2:T(8,128)} copy(f32[129,128,128]{2,1,0:T(8,128)} %fusion.4) | data formatting | bytes 16908288 | tf_op jit(solution)/shard_map/tji,tjr->tir/dot_general | solution.py:54
  321.5 20.1 %fusion.6 = f32[129,128,128]{2,1,0:T(8,128)} fusion(f32[1,129,128,128]{3,2,1,0:T(8,128)} %param.6, f32[129,128,128]{2,1,0:T(8,128)} %gather_fusion, pred[129]{0:T(512)(128)(4,1)S(1)} %compare_and_fusion.1), kind=kOutput, calls=%fused_computation.8 | convolution fusion | flops 3248504832 | bytes 25362560 | tf_op jit(solution)/shard_map/tij,tjr->tir/dot_general | solution.py:48
  341.6 9.5 %copy.37 = f32[129,128,128]{1,0,2:T(8,128)} copy(f32[129,128,128]{2,1,0:T(8,128)} %fusion.6) | data formatting | bytes 16908288 | tf_op jit(solution)/shard_map/tij,tjr->tir/dot_general | solution.py:48
  356.9 7.6 %fusion = f32[31,128,128]{2,0,1:T(8,128)S(1)} fusion(f32[129,128,128]{1,0,2:T(8,128)} %copy.38, f32[129]{0:T(256)S(1)} %and_convert_fusion, s32[129]{0:T(256)S(1)} %bitcast.198), kind=kOutput, calls=%fused_computation.2 | convolution fusion | flops 786243392 | bytes 10486792 | tf_op jit(solution)/shard_map/tc,tbr->cbr/dot_general | solution.py:61
  367.5 8.0 %collective-permute-start.41 = (f32[128,128]{1,0:T(8,128)S(1)}, f32[128,128]{1,0:T(8,128)S(1)}, u32[]{:S(2)}, u32[]{:S(2)}) collective-permute-start(f32[128,128]{1,0:T(8,128)S(1)} %get-tuple-element.28), channel_id=1, source_target_pairs={{0,12},{1,13},{2,14},{3,15},{4,16},{5,17},{6,18},{7,19},{8,20},{9,... | collective-permute-start | bytes 196616 | tf_op jit(solution)/shard_map/ppermute | solution.py:10
  375.5 17.6 %collective-permute-start.40 = (f32[128,128]{1,0:T(8,128)S(1)}, f32[128,128]{1,0:T(8,128)S(1)}, u32[]{:S(2)}, u32[]{:S(2)}) collective-permute-start(f32[128,128]{1,0:T(8,128)S(1)} %get-tuple-element.29), channel_id=1, source_target_pairs={{0,11},{1,12},{2,13},{3,14},{4,15},{5,16},{6,17},{7,18},{8,19},{9,... | collective-permute-start | bytes 196616 | tf_op jit(solution)/shard_map/ppermute | solution.py:10
  398.1 8.4 %collective-permute-start.36 = (f32[128,128]{1,0:T(8,128)S(1)}, f32[128,128]{1,0:T(8,128)S(1)}, u32[]{:S(2)}, u32[]{:S(2)}) collective-permute-start(f32[128,128]{1,0:T(8,128)S(1)} %get-tuple-element.33), channel_id=1, source_target_pairs={{0,7},{1,8},{2,9},{3,10},{4,11},{5,12},{6,13},{7,14},{8,15},{9,16}... | collective-permute-start | bytes 196616 | tf_op jit(solution)/shard_map/ppermute | solution.py:10
  445.7 7.2 %collective-permute-start.44 = (f32[128,128]{1,0:T(8,128)S(1)}, f32[128,128]{1,0:T(8,128)S(1)}, u32[]{:S(2)}, u32[]{:S(2)}) collective-permute-start(f32[128,128]{1,0:T(8,128)S(1)} %get-tuple-element.24), channel_id=1, source_target_pairs={{0,15},{1,16},{2,17},{3,18},{4,19},{5,20},{6,21},{7,22},{8,23},{9,... | collective-permute-start | bytes 196616 | tf_op jit(solution)/shard_map/ppermute | solution.py:10
  462.9 74.3 %all-reduce = (f32[128]{0:T(128)S(1)}, f32[128]{0:T(128)S(1)}) all-reduce(f32[128]{0:T(128)S(1)} %get-tuple-element.4, f32[128]{0:T(128)S(1)} %get-tuple-element.3), channel_id=1, replica_groups=mesh['blk'=256] {'blk'}, use_global_device_ids=true, to_apply=%region_1.0 | all-reduce | flops 256 | bytes 2048 | tf_op jit(solution)/shard_map/psum | solution.py:28
  (151 shorter events, 210.4 us)
Async XLA Ops:
  0.6 276.4 %collective-permute-start.28 = (f32[128,128]{1,0:T(8,128)}, f32[128,128]{1,0:T(8,128)S(1)}, u32[]{:S(2)}, u32[]{:S(2)}) collective-permute-start(f32[128,128]{1,0:T(8,128)} %param.5), channel_id=1, source_target_pairs={{0,32},{1,33},{2,34},{3,35},{4,36},{5,37},{6,38},{7,39},{8,40},{9,... | collective-permute-start | bytes 196616 | tf_op jit(solution)/shard_map/ppermute | solution.py:10
  4.5 272.6 %collective-permute-start.27 = (f32[128,128]{1,0:T(8,128)}, f32[128,128]{1,0:T(8,128)S(1)}, u32[]{:S(2)}, u32[]{:S(2)}) collective-permute-start(f32[128,128]{1,0:T(8,128)} %param.5), channel_id=1, source_target_pairs={{0,48},{1,49},{2,50},{3,51},{4,52},{5,53},{6,54},{7,55},{8,56},{9,... | collective-permute-start | bytes 196616 | tf_op jit(solution)/shard_map/ppermute | solution.py:10
  6.2 270.9 %collective-permute-start.26 = (f32[128,128]{1,0:T(8,128)}, f32[128,128]{1,0:T(8,128)S(1)}, u32[]{:S(2)}, u32[]{:S(2)}) collective-permute-start(f32[128,128]{1,0:T(8,128)} %param.5), channel_id=1, source_target_pairs={{0,64},{1,65},{2,66},{3,67},{4,68},{5,69},{6,70},{7,71},{8,72},{9,... | collective-permute-start | bytes 196616 | tf_op jit(solution)/shard_map/ppermute | solution.py:10
  7.4 269.6 %collective-permute-start.25 = (f32[128,128]{1,0:T(8,128)}, f32[128,128]{1,0:T(8,128)S(1)}, u32[]{:S(2)}, u32[]{:S(2)}) collective-permute-start(f32[128,128]{1,0:T(8,128)} %param.5), channel_id=1, source_target_pairs={{0,80},{1,81},{2,82},{3,83},{4,84},{5,85},{6,86},{7,87},{8,88},{9,... | collective-permute-start | bytes 196616 | tf_op jit(solution)/shard_map/ppermute | solution.py:10
  8.7 16.7 %collective-permute-start = (f32[128,128]{1,0:T(8,128)}, f32[128,128]{1,0:T(8,128)S(1)}, u32[]{:S(2)}, u32[]{:S(2)}) collective-permute-start(f32[128,128]{1,0:T(8,128)} %param.5), channel_id=1, source_target_pairs={{0,255},{1,0},{2,1},{3,2},{4,3},{5,4},{6,5},{7,6},{8,7},{9,8},{10,... | collective-permute-start | bytes 196616 | tf_op jit(solution)/shard_map/ppermute | solution.py:10
  25.4 14.4 %collective-permute-start.1 = (f32[128,128]{1,0:T(8,128)}, f32[128,128]{1,0:T(8,128)S(1)}, u32[]{:S(2)}, u32[]{:S(2)}) collective-permute-start(f32[128,128]{1,0:T(8,128)} %param.5), channel_id=1, source_target_pairs={{0,254},{1,255},{2,0},{3,1},{4,2},{5,3},{6,4},{7,5},{8,6},{9,7},{1... | collective-permute-start | bytes 196616 | tf_op jit(solution)/shard_map/ppermute | solution.py:10
  39.8 16.7 %collective-permute-start.2 = (f32[128,128]{1,0:T(8,128)}, f32[128,128]{1,0:T(8,128)S(1)}, u32[]{:S(2)}, u32[]{:S(2)}) collective-permute-start(f32[128,128]{1,0:T(8,128)} %param.5), channel_id=1, source_target_pairs={{0,253},{1,254},{2,255},{3,0},{4,1},{5,2},{6,3},{7,4},{8,5},{9,6},... | collective-permute-start | bytes 196616 | tf_op jit(solution)/shard_map/ppermute | solution.py:10
  56.5 15.4 %collective-permute-start.3 = (f32[128,128]{1,0:T(8,128)}, f32[128,128]{1,0:T(8,128)S(1)}, u32[]{:S(2)}, u32[]{:S(2)}) collective-permute-start(f32[128,128]{1,0:T(8,128)} %param.5), channel_id=1, source_target_pairs={{0,252},{1,253},{2,254},{3,255},{4,0},{5,1},{6,2},{7,3},{8,4},{9,5... | collective-permute-start | bytes 196616 | tf_op jit(solution)/shard_map/ppermute | solution.py:10
  71.9 18.5 %collective-permute-start.4 = (f32[128,128]{1,0:T(8,128)}, f32[128,128]{1,0:T(8,128)S(1)}, u32[]{:S(2)}, u32[]{:S(2)}) collective-permute-start(f32[128,128]{1,0:T(8,128)} %param.5), channel_id=1, source_target_pairs={{0,251},{1,252},{2,253},{3,254},{4,255},{5,0},{6,1},{7,2},{8,3},{9... | collective-permute-start | bytes 196616 | tf_op jit(solution)/shard_map/ppermute | solution.py:10
  90.4 16.4 %collective-permute-start.5 = (f32[128,128]{1,0:T(8,128)}, f32[128,128]{1,0:T(8,128)S(1)}, u32[]{:S(2)}, u32[]{:S(2)}) collective-permute-start(f32[128,128]{1,0:T(8,128)} %param.5), channel_id=1, source_target_pairs={{0,250},{1,251},{2,252},{3,253},{4,254},{5,255},{6,0},{7,1},{8,2},... | collective-permute-start | bytes 196616 | tf_op jit(solution)/shard_map/ppermute | solution.py:10
  106.8 20.7 %collective-permute-start.6 = (f32[128,128]{1,0:T(8,128)}, f32[128,128]{1,0:T(8,128)S(1)}, u32[]{:S(2)}, u32[]{:S(2)}) collective-permute-start(f32[128,128]{1,0:T(8,128)} %param.5), channel_id=1, source_target_pairs={{0,249},{1,250},{2,251},{3,252},{4,253},{5,254},{6,255},{7,0},{8,1... | collective-permute-start | bytes 196616 | tf_op jit(solution)/shard_map/ppermute | solution.py:10
  127.5 18.2 %collective-permute-start.7 = (f32[128,128]{1,0:T(8,128)}, f32[128,128]{1,0:T(8,128)S(1)}, u32[]{:S(2)}, u32[]{:S(2)}) collective-permute-start(f32[128,128]{1,0:T(8,128)} %param.5), channel_id=1, source_target_pairs={{0,248},{1,249},{2,250},{3,251},{4,252},{5,253},{6,254},{7,255},{8... | collective-permute-start | bytes 196616 | tf_op jit(solution)/shard_map/ppermute | solution.py:10
  145.7 16.8 %collective-permute-start.8 = (f32[128,128]{1,0:T(8,128)}, f32[128,128]{1,0:T(8,128)S(1)}, u32[]{:S(2)}, u32[]{:S(2)}) collective-permute-start(f32[128,128]{1,0:T(8,128)} %param.5), channel_id=1, source_target_pairs={{0,247},{1,248},{2,249},{3,250},{4,251},{5,252},{6,253},{7,254},{8... | collective-permute-start | bytes 196616 | tf_op jit(solution)/shard_map/ppermute | solution.py:10
  162.5 16.8 %collective-permute-start.9 = (f32[128,128]{1,0:T(8,128)}, f32[128,128]{1,0:T(8,128)S(1)}, u32[]{:S(2)}, u32[]{:S(2)}) collective-permute-start(f32[128,128]{1,0:T(8,128)} %param.5), channel_id=1, source_target_pairs={{0,246},{1,247},{2,248},{3,249},{4,250},{5,251},{6,252},{7,253},{8... | collective-permute-start | bytes 196616 | tf_op jit(solution)/shard_map/ppermute | solution.py:10
  366.8 26.3 %collective-permute-start.31 = (f32[128,128]{1,0:T(8,128)S(1)}, f32[128,128]{1,0:T(8,128)S(1)}, u32[]{:S(2)}, u32[]{:S(2)}) collective-permute-start(f32[128,128]{1,0:T(8,128)S(1)} %get-tuple-element.27), channel_id=1, source_target_pairs={{0,2},{1,3},{2,4},{3,5},{4,6},{5,7},{6,8},{7,9},{8,10},{9,11},{10,... | collective-permute-start | bytes 196616 | tf_op jit(solution)/shard_map/ppermute | solution.py:10
  367.5 30.6 %collective-permute-start.41 = (f32[128,128]{1,0:T(8,128)S(1)}, f32[128,128]{1,0:T(8,128)S(1)}, u32[]{:S(2)}, u32[]{:S(2)}) collective-permute-start(f32[128,128]{1,0:T(8,128)S(1)} %get-tuple-element.28), channel_id=1, source_target_pairs={{0,12},{1,13},{2,14},{3,15},{4,16},{5,17},{6,18},{7,19},{8,20},{9,... | collective-permute-start | bytes 196616 | tf_op jit(solution)/shard_map/ppermute | solution.py:10
  375.5 31.0 %collective-permute-start.40 = (f32[128,128]{1,0:T(8,128)S(1)}, f32[128,128]{1,0:T(8,128)S(1)}, u32[]{:S(2)}, u32[]{:S(2)}) collective-permute-start(f32[128,128]{1,0:T(8,128)S(1)} %get-tuple-element.29), channel_id=1, source_target_pairs={{0,11},{1,12},{2,13},{3,14},{4,15},{5,16},{6,17},{7,18},{8,19},{9,... | collective-permute-start | bytes 196616 | tf_op jit(solution)/shard_map/ppermute | solution.py:10
  393.1 16.6 %collective-permute-start.39 = (f32[128,128]{1,0:T(8,128)S(1)}, f32[128,128]{1,0:T(8,128)S(1)}, u32[]{:S(2)}, u32[]{:S(2)}) collective-permute-start(f32[128,128]{1,0:T(8,128)S(1)} %get-tuple-element.30), channel_id=1, source_target_pairs={{0,10},{1,11},{2,12},{3,13},{4,14},{5,15},{6,16},{7,17},{8,18},{9,... | collective-permute-start | bytes 196616 | tf_op jit(solution)/shard_map/ppermute | solution.py:10
  393.1 22.4 %collective-permute-start.38 = (f32[128,128]{1,0:T(8,128)S(1)}, f32[128,128]{1,0:T(8,128)S(1)}, u32[]{:S(2)}, u32[]{:S(2)}) collective-permute-start(f32[128,128]{1,0:T(8,128)S(1)} %get-tuple-element.31), channel_id=1, source_target_pairs={{0,9},{1,10},{2,11},{3,12},{4,13},{5,14},{6,15},{7,16},{8,17},{9,1... | collective-permute-start | bytes 196616 | tf_op jit(solution)/shard_map/ppermute | solution.py:10
  393.1 22.8 %collective-permute-start.37 = (f32[128,128]{1,0:T(8,128)S(1)}, f32[128,128]{1,0:T(8,128)S(1)}, u32[]{:S(2)}, u32[]{:S(2)}) collective-permute-start(f32[128,128]{1,0:T(8,128)S(1)} %get-tuple-element.32), channel_id=1, source_target_pairs={{0,8},{1,9},{2,10},{3,11},{4,12},{5,13},{6,14},{7,15},{8,16},{9,17... | collective-permute-start | bytes 196616 | tf_op jit(solution)/shard_map/ppermute | solution.py:10
  398.1 17.9 %collective-permute-start.36 = (f32[128,128]{1,0:T(8,128)S(1)}, f32[128,128]{1,0:T(8,128)S(1)}, u32[]{:S(2)}, u32[]{:S(2)}) collective-permute-start(f32[128,128]{1,0:T(8,128)S(1)} %get-tuple-element.33), channel_id=1, source_target_pairs={{0,7},{1,8},{2,9},{3,10},{4,11},{5,12},{6,13},{7,14},{8,15},{9,16}... | collective-permute-start | bytes 196616 | tf_op jit(solution)/shard_map/ppermute | solution.py:10
  406.6 12.5 %collective-permute-start.35 = (f32[128,128]{1,0:T(8,128)S(1)}, f32[128,128]{1,0:T(8,128)S(1)}, u32[]{:S(2)}, u32[]{:S(2)}) collective-permute-start(f32[128,128]{1,0:T(8,128)S(1)} %get-tuple-element.34), channel_id=1, source_target_pairs={{0,6},{1,7},{2,8},{3,9},{4,10},{5,11},{6,12},{7,13},{8,14},{9,15},... | collective-permute-start | bytes 196616 | tf_op jit(solution)/shard_map/ppermute | solution.py:10
  416.0 12.5 %collective-permute-start.30 = (f32[128,128]{1,0:T(8,128)S(1)}, f32[128,128]{1,0:T(8,128)S(1)}, u32[]{:S(2)}, u32[]{:S(2)}) collective-permute-start(f32[128,128]{1,0:T(8,128)S(1)} %get-tuple-element.8), channel_id=1, source_target_pairs={{0,1},{1,2},{2,3},{3,4},{4,5},{5,6},{6,7},{7,8},{8,9},{9,10},{10,1... | collective-permute-start | bytes 196616 | tf_op jit(solution)/shard_map/ppermute | solution.py:10
  438.8 14.2 %collective-permute-start.48 = (f32[128,128]{1,0:T(8,128)S(1)}, f32[128,128]{1,0:T(8,128)S(1)}, u32[]{:S(2)}, u32[]{:S(2)}) collective-permute-start(f32[128,128]{1,0:T(8,128)S(1)} %get-tuple-element.20), channel_id=1, source_target_pairs={{0,64},{1,65},{2,66},{3,67},{4,68},{5,69},{6,70},{7,71},{8,72},{9,... | collective-permute-start | bytes 196616 | tf_op jit(solution)/shard_map/ppermute | solution.py:10
  (37 other events, 511.2 us)
where the time goes:
time: 547 us; the launch traced here: 538 us
  starting transfers between devices  257 us (47%)
  waiting for transfers between devices  120 us (22%)
  blocking collectives  74.3 us (14%)
  matrix products  53.2 us (10%)
  local copies, waits for them, and re-layouts  29.8 us (5%)
    ppermute x60, starting transfers between devices, shifted(): return lax.ppermute(value, axis, pairs)  257 us
    ppermute x60, waiting for transfers between devices, shifted(): return lax.ppermute(value, axis, pairs)  120 us
    psum x1, blocking collectives, column_total(): return lax.psum(jnp.sum(values, axis=0), 'blk')  74.3 us
    dot_general x1, matrix products, per_device(): jnp.einsum('tij,tjr->tir', own_tiles, jnp.take(blocks, route_pairs[:, 1],...  20.1 us
    dot_general x1, matrix products, per_device(): jnp.einsum('tji,tjr->tir', own_tiles, jnp.take(blocks, route_pairs[:, 0],...  19.8 us
  transfers between devices with their start and end apart: 60, of which 34 were waited for; matrix products, arithmetic and copies ran while one was open for 0% of the time, Pallas kernels for 0%

commit v1 on v0

v1 whole, which is shorter than its diff:
```python
import functools

import jax
import jax.numpy as jnp
from jax import lax
from jax.experimental import pallas as pl
from jax.experimental.pallas import tpu as pltpu
from jax.sharding import PartitionSpec as P

MESH = pl.DeviceIdType.MESH
NB = 256
B = 128
NT = 129
NC = 31
CHUNKS = 8
HALF = B // 2
F32 = jnp.float32
BF16 = jnp.bfloat16


def split_pair(value):
    high = value.astype(BF16)
    low = (value - high.astype(F32)).astype(BF16)
    return high, low


def cg_kernel(
    rp, x_ref, tiles, sol_ref, res_ref,
    tf, tb, xs, wb, part, prods, rel_in, cross_in, axis_in, half_a, half_b, v_out, v_mid, v_near, v_far,
    tile_sem, g_send, g_recv, c_send, c_recv, ax_send, ax_recv, ha_send, ha_recv, hb_send, hb_recv,
    s_send, s_recv, d_send, d_recv, ox_send, ox_recv, pa_send, pa_recv, pb_send, pb_recv,
    n_send, n_recv, f_send, f_recv,
):
    me = lax.axis_index("blk")
    par = lax.rem(me, 2)
    partner = me + 1 - 2 * par
    col = me // 16
    px = me // 64
    py = lax.rem(col, 4)

    def near(step):
        return lax.rem(me + step + NB, NB)

    def at_x(step):
        return me + (lax.rem(px + step, 4) - px) * 64

    def at_y(step):
        return me + (lax.rem(py + step, 4) - py) * 16

    def slot(dx, dy, tx, ty):
        owner_col = lax.rem(px + dx, 4) * 4 + lax.rem(py + dy, 4)
        there_col = lax.rem(px + tx, 4) * 4 + lax.rem(py + ty, 4)
        return 15 + lax.rem(owner_col - there_col + 16, 16)

    def remote(src, dst, send_sem, recv_sem, device):
        return pltpu.make_async_remote_copy(
            src_ref=src, dst_ref=dst, send_sem=send_sem, recv_sem=recv_sem,
            device_id=(device,), device_id_type=MESH,
        )

    bounds = [NT * q // CHUNKS for q in range(CHUNKS + 1)]
    tile_copies = []
    for q in range(CHUNKS):
        span = pl.ds(bounds[q], bounds[q + 1] - bounds[q])
        copy = pltpu.make_async_copy(tiles.at[0, span], tf.at[span], tile_sem.at[q])
        copy.start()
        tile_copies.append(copy)

    barrier = pltpu.get_barrier_semaphore()
    axis_devices = [at_x(d) for d in (1, 2, 3)] + [at_y(d) for d in (1, 2, 3)]
    for device in axis_devices + [near(2), near(4), near(12), near(14), near(-2), partner]:
        pl.semaphore_signal(barrier, inc=1, device_id=(device,), device_id_type=MESH)
    pl.semaphore_wait(barrier, 12)

    sends = []

    def go(copy):
        copy.start()
        sends.append(copy)

    for d in (1, 2, 3):
        go(remote(x_ref, xs.at[slot(0, 0, 0, d)], ax_send.at[2 + d], ax_recv.at[2 + d], at_y(d)))
        go(remote(x_ref, xs.at[slot(0, 0, d, 0)], ax_send.at[d - 1], ax_recv.at[d - 1], at_x(d)))
    for r in (2, 4, 14, 12):
        go(remote(x_ref, xs.at[r], g_send.at[r // 2 - 1], g_recv.at[r // 2 - 1], near(-r)))
    xs[0] = x_ref[...]

    def split_tile(t, carry):
        value = tf[t]
        high, low = split_pair(value)
        tb[t, 0, :, 0:B] = high
        tb[t, 0, :, B : 2 * B] = low
        high, low = split_pair(value.T)
        tb[t, 1, :, 0:B] = high
        tb[t, 1, :, B : 2 * B] = low
        return carry

    def prepare(q):
        tile_copies[q].wait()
        lax.fori_loop(bounds[q], bounds[q + 1], split_tile, 0)

    def arrive_near(r):
        remote(x_ref, xs.at[r], g_send.at[r // 2 - 1], g_recv.at[r // 2 - 1], near(-r)).wait_recv()

    def cross(r):
        place = r // 2 - 1 + par
        go(remote(xs.at[r], xs.at[r - 1 + 2 * par], c_send.at[place], c_recv.at[place], partner))

    for q in range(4):
        prepare(q)

    arrive_near(4)
    go(remote(xs.at[4], xs.at[6], g_send.at[2], g_recv.at[2], near(-2)))
    go(remote(xs.at[4], xs.at[8], g_send.at[3], g_recv.at[3], near(-4)))
    arrive_near(12)
    go(remote(xs.at[12], xs.at[10], g_send.at[4], g_recv.at[4], near(2)))
    for e in (1, 2, 3):
        src = slot(e, 0, 0, 0)
        remote(x_ref, xs.at[src], ax_send.at[3 - e], ax_recv.at[3 - e], partner).wait_recv()
        for d in (1, 2, 3):
            place = 3 * (e - 1) + d - 1
            rows = pl.ds(0, HALF)
            go(remote(xs.at[src, rows], xs.at[slot(e, 0, 0, d), rows], ha_send.at[place], ha_recv.at[place], at_y(d)))
        src = slot(0, e, 0, 0)
        remote(x_ref, xs.at[src], ax_send.at[6 - e], ax_recv.at[6 - e], partner).wait_recv()
        for d in (1, 2, 3):
            place = 3 * (e - 1) + d - 1
            rows = pl.ds(HALF, HALF)
            go(remote(xs.at[src, rows], xs.at[slot(0, e, d, 0), rows], hb_send.at[place], hb_recv.at[place], at_x(d)))
    for r in (4, 12):
        cross(r)
    for r in (2, 14):
        arrive_near(r)
        cross(r)
    for q in range(4, CHUNKS):
        prepare(q)
    for r in (6, 10, 8):
        arrive_near(r)
        cross(r)
    for e in (1, 2, 3):
        for d in (1, 2, 3):
            place = 3 * (e - 1) + d - 1
            rows = pl.ds(0, HALF)
            dst = xs.at[slot(e, 4 - d, 0, 0), rows]
            remote(dst, dst, ha_send.at[place], ha_recv.at[place], partner).wait_recv()
            rows = pl.ds(HALF, HALF)
            dst = xs.at[slot(4 - d, e, 0, 0), rows]
            remote(dst, dst, hb_send.at[place], hb_recv.at[place], partner).wait_recv()
    go(remote(xs.at[16 - 16 * par], xs.at[15 - 14 * par], c_send.at[7 - 7 * par], c_recv.at[7 - 7 * par], partner))
    for i in range(8):
        dst = xs.at[2 * i + 1]
        remote(dst, dst, c_send.at[i], c_recv.at[i], partner).wait_recv()

    def split_block(c, carry):
        high, low = split_pair(xs[c])
        wb[c, 0:B, 0:B] = high
        wb[c, 0:B, B : 2 * B] = low
        wb[c, B : 2 * B, 0:B] = high
        wb[c, B : 2 * B, B : 2 * B] = low
        return carry

    lax.fori_loop(0, NC, split_block, 0)

    def product(t, turn, c):
        both = jnp.dot(tb[t, turn], wb[c], preferred_element_type=F32)
        return both[:, 0:B] + both[:, B : 2 * B]

    def near_tile(i, carry):
        for u in range(3):
            place = 3 * i + u
            t = jnp.where(place < 16, place, 16 * (place - 15))
            prods[place, 0] = product(t, 0, rp[t, 1])
            prods[place, 1] = product(t, 1, rp[t, 0])
        return carry

    lax.fori_loop(0, 8, near_tile, 0)

    def as_mask(flag):
        return flag.astype(jnp.int32).astype(F32)

    def place_all(c, carry):
        part[c] = as_mask(rp[0, 0] == c) * prods[0, 0]
        return carry

    lax.fori_loop(0, NC, place_all, 0)

    def place_small(c, carry):
        total = part[c]
        for u in range(16):
            by_row = u < 16 - c
            t = jnp.where(by_row, u + 1, u + c - 15)
            safe = jnp.minimum(t, 15)
            start = rp[safe, 0]
            hit = jnp.where(by_row, start, start + safe) == c
            mask = as_mask(hit) * as_mask(t < 16)
            total = total + mask * prods[safe, jnp.where(by_row, 0, 1)]
        part[c] = total
        return carry

    lax.fori_loop(0, 17, place_small, 0)

    def place_large(l, carry):
        c = jnp.where(l == 0, 0, 15 + l)
        total = part[c]
        for m in range(1, 9):
            total = total + as_mask(rp[16 * m, 0] == c) * prods[15 + m, 0]
            if m < 8:
                total = total + as_mask(rp[16 * m, 1] == c) * prods[15 + m, 1]
        part[c] = total
        return carry

    lax.fori_loop(0, 16, place_large, 0)

    def far_tiles(j, carry):
        first = jnp.zeros((B, B), F32)
        second = jnp.zeros((B, B), F32)
        for k in range(2, 9):
            t = 16 * k - j
            ahead = rp[t, 0] == j
            small = jnp.where(ahead, j, 16 - j)
            large = jnp.where(ahead, 15 + k, 32 - k)
            turn = jnp.where(ahead, 0, 1)
            mask = as_mask(ahead)
            to_small = product(t, turn, large)
            to_large = product(t, 1 - turn, small)
            kept = mask * to_small
            first = first + kept
            second = second + (1.0 - mask) * to_small
            part[15 + k] += mask * to_large
            part[32 - k] += (1.0 - mask) * to_large
        part[j] += first
        part[16 - j] += second
        return carry

    lax.fori_loop(1, 16, far_tiles, 0)

    def fold_rows(value):
        total = value[0:8]
        for q in range(1, B // 8):
            total = total + value[8 * q : 8 * q + 8]
        return total

    def add_inner(c, carry):
        return carry + fold_rows(xs[c] * part[c])

    inner = lax.fori_loop(0, NC, add_inner, jnp.zeros((8, B), F32))
    own = x_ref[...]
    norm = jnp.sum(fold_rows(own * own), axis=0, keepdims=True)
    inner = jnp.sum(inner, axis=0, keepdims=True)
    row_ids = lax.broadcasted_iota(jnp.int32, (8, B), 0)
    v_out[...] = jnp.where(row_ids == 0, inner, jnp.where(row_ids == 1, norm, 0.0))
    for k in range(1, 16):
        go(remote(v_out, v_near.at[k - 1], n_send.at[k - 1], n_recv.at[k - 1], near(k)))

    for i in range(8):
        go(remote(part.at[2 * i + 1], cross_in.at[i], ox_send.at[i], ox_recv.at[i], partner))
    def send_halves(e, d):
        place = 3 * (e - 1) + d - 1
        rows = pl.ds(0, HALF)
        go(remote(part.at[slot(e, d, 0, 0), rows], half_a.at[place], pa_send.at[place], pa_recv.at[place], at_y(d)))
        rows = pl.ds(HALF, HALF)
        go(remote(part.at[slot(d, e, 0, 0), rows], half_b.at[place], pb_send.at[place], pb_recv.at[place], at_x(d)))

    for e in (1, 2, 3):
        for d in (1, 2, 3):
            if e + d > 2:
                send_halves(e, d)
    for i in range(8):
        remote(cross_in.at[i], cross_in.at[i], ox_send.at[i], ox_recv.at[i], partner).wait_recv()

    def merge(i):
        c = 2 * i + 2 - 2 * par
        part[c] += cross_in[i]

    def add_cross(i, carry):
        merge(i)
        return carry

    lax.fori_loop(0, 8, add_cross, 0)
    send_halves(1, 1)
    go(remote(part.at[8], rel_in.at[0], s_send.at[0], s_recv.at[0], near(4)))
    go(remote(part.at[6], rel_in.at[1], s_send.at[1], s_recv.at[1], near(2)))
    go(remote(part.at[10], rel_in.at[2], s_send.at[2], s_recv.at[2], near(-2)))
    go(remote(part.at[2], rel_in.at[3], s_send.at[3], s_recv.at[3], near(2)))
    go(remote(part.at[14], rel_in.at[4], s_send.at[4], s_recv.at[4], near(14)))

    for k in range(15):
        remote(v_out, v_near.at[k], n_send.at[k], n_recv.at[k], partner).wait_recv()
    mid = v_out[...]
    for k in range(15):
        mid = mid + v_near[k]
    v_mid[...] = mid
    for k in range(1, 16):
        go(remote(v_mid, v_far.at[k - 1], f_send.at[k - 1], f_recv.at[k - 1], near(16 * k)))

    for e in (1, 2, 3):
        at = slot(e, 0, 0, 0)
        for d in (1, 2, 3):
            place = 3 * (e - 1) + d - 1
            remote(half_a.at[place], half_a.at[place], pa_send.at[place], pa_recv.at[place], partner).wait_recv()
            part[at, 0:HALF] += half_a[place]
        go(remote(part.at[at], axis_in.at[e - 1], d_send.at[e - 1], d_recv.at[e - 1], at_x(e)))
        at = slot(0, e, 0, 0)
        for d in (1, 2, 3):
            place = 3 * (e - 1) + d - 1
            remote(half_b.at[place], half_b.at[place], pb_send.at[place], pb_recv.at[place], partner).wait_recv()
            part[at, HALF:B] += half_b[place]
        go(remote(part.at[at], axis_in.at[2 + e], d_send.at[2 + e], d_recv.at[2 + e], at_y(e)))
    for i in range(3):
        remote(rel_in.at[i], rel_in.at[i], s_send.at[i], s_recv.at[i], partner).wait_recv()
    part[4] += rel_in[0] + rel_in[1]
    go(remote(part.at[4], rel_in.at[5], s_send.at[5], s_recv.at[5], near(4)))
    part[12] += rel_in[2]
    go(remote(part.at[12], rel_in.at[6], s_send.at[6], s_recv.at[6], near(12)))

    for k in range(15):
        remote(v_mid, v_far.at[k], f_send.at[k], f_recv.at[k], partner).wait_recv()
    total = v_mid[...]
    for k in range(15):
        total = total + v_far[k]
    step = total[1:2] / total[0:1]

    for i in range(3, 7):
        remote(rel_in.at[i], rel_in.at[i], s_send.at[i], s_recv.at[i], partner).wait_recv()
    for i in range(6):
        remote(axis_in.at[i], axis_in.at[i], d_send.at[i], d_recv.at[i], partner).wait_recv()
    image = part[0]
    for i in range(3, 7):
        image = image + rel_in[i]
    for i in range(6):
        image = image + axis_in[i]
    sol_ref[...] = step * own
    res_ref[...] = own - step * image
    for copy in sends:
        copy.wait_send()


def per_device(right_side, kernel_tiles, route_pairs):
    vmem = pltpu.VMEM
    dma = pltpu.SemaphoreType.DMA
    counts = [7, 8, 6, 9, 9, 7, 6, 8, 9, 9, 15, 15]
    sems = []
    for count in counts:
        sems += [dma((count,)), dma((count,))]
    out = jax.ShapeDtypeStruct((B, B), F32)
    whole = pl.BlockSpec(memory_space=vmem)
    return pl.pallas_call(
        cg_kernel,
        out_shape=(out, out),
        in_specs=[pl.BlockSpec(memory_space=pltpu.SMEM), whole, pl.BlockSpec(memory_space=pl.ANY)],
        out_specs=(whole, whole),
        scratch_shapes=[
            vmem((NT, B, B), F32),
            vmem((NT, 2, B, 2 * B), BF16),
            vmem((NC, B, B), F32),
            vmem((NC, 2 * B, 2 * B), BF16),
            vmem((NC, B, B), F32),
            vmem((24, 2, B, B), F32),
            vmem((7, B, B), F32),
            vmem((8, B, B), F32),
            vmem((6, B, B), F32),
            vmem((9, HALF, B), F32),
            vmem((9, HALF, B), F32),
            vmem((8, B), F32),
            vmem((8, B), F32),
            vmem((15, 8, B), F32),
            vmem((15, 8, B), F32),
            dma((CHUNKS,)),
        ]
        + sems,
        compiler_params=pltpu.CompilerParams(
            collective_id=0, has_side_effects=True, vmem_limit_bytes=60 * 1024 * 1024
        ),
    )(route_pairs, right_side, kernel_tiles)


def solution(mesh):
    return jax.shard_map(
        per_device,
        mesh=mesh,
        in_specs=(P("blk", None), P("blk", None, None, None), P()),
        out_specs=(P("blk", None), P("blk", None)),
        check_vma=False,
    )
```

time: 547 us -> 72.8 us (0.13); the launches traced: 538 us -> 72.5 us
  starting transfers between devices: 257 us -> 0 us
  waiting for transfers between devices: 120 us -> 0 us
  blocking collectives: 74.3 us -> 0 us
  Pallas kernels: 0 us -> 67.6 us
  matrix products: 53.2 us -> 0 us
  local copies, waits for them, and re-layouts: 29.8 us -> 4.35 us
    ppermute x60 -> x0, starting transfers between devices: 257 us -> none  [shifted(): return lax.ppermute(value, axis, pairs)]
    ppermute x60 -> x0, waiting for transfers between devices: 120 us -> none  [shifted(): return lax.ppermute(value, axis, pairs)]
    psum x1 -> x0, blocking collectives: 74.3 us -> none  [column_total(): return lax.psum(jnp.sum(values, axis=0), 'blk')]
    pallas_call x0 -> x1, Pallas kernels: none -> 67.6 us  [per_device(): pl.pallas_call(cg_kernel, out_shape=(out, out), in_specs=[pl.BlockSpec(me...]
    dot_general x4 -> x0, matrix products: 53.2 us -> none  [the longest x1 20.1 us: per_device(): jnp.einsum('tij,tjr->tir', own_tiles, jnp.take(blocks, route_pairs[:, 1],...]
    dot_general x2 -> x0, local copies, waits for them, and re-layouts: 19 us -> none  [the longest x1 9.53 us: per_device(): jnp.einsum('tij,tjr->tir', own_tiles, jnp.take(blocks, route_pairs[:, 1],...]
    gather x2 -> x0, local copies, waits for them, and re-layouts: 8.86 us -> none  [the longest x1 4.43 us: per_device(): jnp.take(blocks, route_pairs[:, 1], axis=0)]
  transfers between devices with their start and end apart: 60 -> 0, of which waited for: 34 -> 0; matrix products, arithmetic and copies ran while one was open for 0% -> 0% of each run, Pallas kernels for 0% -> 0%
where the time goes in v1:
time: 72.8 us; the launch traced here: 72.5 us
  Pallas kernels  67.6 us (93%)
  local copies, waits for them, and re-layouts  4.35 us (6%)
    pallas_call x1, Pallas kernels, per_device(): pl.pallas_call(cg_kernel, out_shape=(out, out), in_specs=[pl.BlockSpec(me...  67.6 us
    unnamed x3, local copies, waits for them, and re-layouts  4.35 us

profile of v1, /device:TPU:1, one launch (start us, length us, event | category | flops | bytes accessed | tf_op | source)
XLA Modules:
  0.0 72.5 jit_solution(6698751238459459942)
XLA Ops:
  0.6 1.4 %copy.5.rp = s32[129,2]{1,0:T(8,128)} copy(s32[129,2]{0,1:T(2,128)} %param.5) | data formatting | bytes 2064 | tf_op args[2]
  2.0 67.6 %shard_map.50 = (f32[128,128]{1,0:T(8,128)}, f32[128,128]{1,0:T(8,128)}) custom-call(s32[129,2]{1,0:T(8,128)} %copy.5.rp, f32[128,128]{1,0:T(8,128)} %x_ref.1, f32[1,129,128,128]{3,2,1,0:T(8,128)} %tiles.1), custom_call_target="tpu_custom_call" | custom-call | tf_op jit(solution)/shard_map/pallas_call | solution.py:347
  69.6 1.5 %copy.8 = f32[128,128]{1,0:T(8,128)} copy(f32[128,128]{1,0:T(8,128)} %get-tuple-element.4) | data formatting | bytes 131072
  71.1 1.5 %copy.9 = f32[128,128]{1,0:T(8,128)} copy(f32[128,128]{1,0:T(8,128)} %get-tuple-element.5) | data formatting | bytes 131072

commit v2 on v0

v2 whole, which is shorter than its diff:
```python
import functools

import jax
import jax.numpy as jnp
from jax import lax
from jax.experimental import pallas as pl
from jax.experimental.pallas import tpu as pltpu
from jax.sharding import PartitionSpec as P

MESH = pl.DeviceIdType.MESH
NB = 256
B = 128
NT = 129
NC = 31
CHUNK = 16
CHUNKS = 9
HALF = B // 2
F32 = jnp.float32
BF16 = jnp.bfloat16


def split_pair(value):
    high = value.astype(BF16)
    low = (value - high.astype(F32)).astype(BF16)
    return high, low


def sort_network(count):
    pairs = []
    p = 1
    while p < count:
        k = p
        while k >= 1:
            for j in range(k % p, count - k, 2 * k):
                for i in range(min(k, count - j - k)):
                    if (i + j) // (2 * p) == (i + j + k) // (2 * p):
                        pairs.append((i + j, i + j + k))
            k //= 2
        p *= 2
    return pairs


def cg_kernel(
    rp, x_ref, tiles, image_ref, step_ref,
    tf, tb, xs, wb, part, wide, tight, wide_runs, tight_runs,
    cross_in, relay_in, near_in, axis_in, half_a, half_b,
    v_out, v_mid, v_near, v_far, wide_keys, tight_keys, wide_last, tight_last,
    tile_sem, sent, g_recv, first_recv, block_recv, cross_recv, back_recv, relay_recv, half_recv, end_recv, sum_recv,
):
    me = lax.axis_index("blk")
    par = lax.rem(me, 2)
    partner = me + 1 - 2 * par
    col = me // 16
    px = me // 64
    py = lax.rem(col, 4)

    def near(step):
        return lax.rem(me + step + NB, NB)

    def at_x(step):
        return me + (lax.rem(px + step, 4) - px) * 64

    def at_y(step):
        return me + (lax.rem(py + step, 4) - py) * 16

    def slot(dx, dy, tx, ty):
        owner_col = lax.rem(px + dx, 4) * 4 + lax.rem(py + dy, 4)
        there_col = lax.rem(px + tx, 4) * 4 + lax.rem(py + ty, 4)
        return 15 + lax.rem(owner_col - there_col + 16, 16)

    def remote(src, dst, send_sem, recv_sem, device):
        return pltpu.make_async_remote_copy(
            src_ref=src, dst_ref=dst, send_sem=send_sem, recv_sem=recv_sem,
            device_id=(device,), device_id_type=MESH,
        )

    def arrive(dst, recv_sem):
        remote(dst, dst, sent.at[0], recv_sem, partner).wait_recv()

    half = [pl.ds(0, HALF), pl.ds(HALF, HALF)]
    low_half, high_half = half
    halves_sent = [0] * 8

    def go(group, halves, src, dst, recv_sem, device):
        halves_sent[group] += halves
        remote(src, dst, sent.at[group], recv_sem, device).start()

    def tile_copy(q, count):
        span = pl.ds(q * CHUNK, count)
        return pltpu.make_async_copy(tiles.at[0, span], tf.at[span], tile_sem.at[q])

    for q in range(CHUNKS - 1):
        tile_copy(q, CHUNK).start()
    tile_copy(CHUNKS - 1, 1).start()

    barrier = pltpu.get_barrier_semaphore()
    axis_devices = [at_x(d) for d in (1, 2, 3)] + [at_y(d) for d in (1, 2, 3)]
    for device in axis_devices + [near(2), near(4), near(12), near(14), near(-2), partner]:
        pl.semaphore_signal(barrier, inc=1, device_id=(device,), device_id_type=MESH)
    def ordered(keys, count):
        keys = list(keys)
        for lower, upper in sort_network(count):
            if upper < len(keys):
                small, big = jnp.minimum(keys[lower], keys[upper]), jnp.maximum(keys[lower], keys[upper])
                keys[lower], keys[upper] = small, big
        return keys

    keys = [rp[0, 16 * m] * 32 + m - 1 for m in range(1, 9)]
    keys += [rp[1, 16 * m] * 32 + m + 7 for m in range(1, 8)]
    for i, key in enumerate(ordered(keys, 16)):
        wide_keys[i] = key
    keys = [rp[0, t] * 32 + t for t in range(16)] + [rp[1, t] * 32 + t + 15 for t in range(1, 16)]
    for i, key in enumerate(ordered(keys, 32)):
        tight_keys[i] = key

    def find_last(c, carry):
        for keys, last, count in ((wide_keys, wide_last, 15), (tight_keys, tight_last, 31)):
            found = jnp.int32(-1)
            for i in range(count):
                found = found + (keys[i] < (c + 1) * 32).astype(jnp.int32)
            ends_here = lax.div(keys[jnp.maximum(found, 0)], 32) == c
            last[c] = jnp.where(ends_here, found, count)
        return carry

    lax.fori_loop(0, NC, find_last, 0)

    pl.semaphore_wait(barrier, 12)

    def first_x(d, h):
        sem = first_recv.at[d - 1] if h == 0 else block_recv
        go(0, 1, x_ref.at[half[h]], xs.at[slot(0, 0, d, 0), half[h]], sem, at_x(d))

    def first_y(d, h):
        sem = first_recv.at[2 + d] if h == 1 else block_recv
        go(0, 1, x_ref.at[half[h]], xs.at[slot(0, 0, 0, d), half[h]], sem, at_y(d))

    for h in (0, 1):
        go(1, 1, x_ref.at[half[h]], xs.at[4, half[h]], g_recv.at[h], near(-4))
        go(1, 1, x_ref.at[half[h]], xs.at[12, half[h]], g_recv.at[2 + h], near(-12))
    for d in (2, 1, 3):
        first_x(d, 0)
        first_y(d, 1)
    xs[0] = x_ref[...]

    def split_tile(t):
        high, low = split_pair(tf[t])
        tb[t, 0, :, 0:B] = high
        tb[t, 0, :, B : 2 * B] = low
        tb[t, 1, :, 0:B] = high.T
        tb[t, 1, :, B : 2 * B] = low.T

    def prepare(q, carry):
        tile_copy(q, CHUNK).wait()
        for u in range(CHUNK):
            split_tile(q * CHUNK + u)
        return carry

    def cross(r):
        go(2, 2, xs.at[r], xs.at[r - 1 + 2 * par], cross_recv, partner)

    lax.fori_loop(0, 3, prepare, 0)
    go(1, 2, x_ref, xs.at[2], g_recv.at[4], near(-2))
    go(1, 2, x_ref, xs.at[14], g_recv.at[5], near(-14))
    for d in (1, 3, 2):
        first_x(d, 1)
        first_y(d, 0)
    lax.fori_loop(3, CHUNKS - 1, prepare, 0)
    tile_copy(CHUNKS - 1, 1).wait()
    split_tile(NT - 1)

    def forward(e):
        src = slot(e, 0, 0, 0)
        arrive(xs.at[src, low_half], first_recv.at[3 - e])
        for d in (2, 1, 3):
            go(3, 1, xs.at[src, low_half], xs.at[slot(e, 0, 0, d), low_half], block_recv, at_y(d))
        src = slot(0, e, 0, 0)
        arrive(xs.at[src, high_half], first_recv.at[6 - e])
        for d in (2, 1, 3):
            go(3, 1, xs.at[src, high_half], xs.at[slot(0, e, d, 0), high_half], block_recv, at_x(d))

    def forward_near(h):
        arrive(xs.at[4, half[h]], g_recv.at[h])
        go(1, 1, xs.at[4, half[h]], xs.at[8, half[h]], g_recv.at[6], near(-4))
        go(1, 1, xs.at[4, half[h]], xs.at[6, half[h]], g_recv.at[7], near(-2))
        arrive(xs.at[12, half[h]], g_recv.at[2 + h])
        go(1, 1, xs.at[12, half[h]], xs.at[10, half[h]], g_recv.at[8], near(2))

    forward(1)
    forward(3)
    forward_near(0)
    forward(2)
    forward_near(1)
    for r in (4, 12):
        cross(r)
    for r, q in ((2, 4), (14, 5)):
        arrive(xs.at[r], g_recv.at[q])
        cross(r)

    def split_block(c, carry):
        high, low = split_pair(xs[c])
        wb[c, 0:B, 0:B] = high
        wb[c, 0:B, B : 2 * B] = low
        wb[c, B : 2 * B, 0:B] = high
        wb[c, B : 2 * B, B : 2 * B] = low
        return carry

    def product(t, turn, c):
        both = jnp.dot(tb[t, turn], wb[c], preferred_element_type=F32)
        return both[:, 0:B] + both[:, B : 2 * B]

    def as_mask(flag):
        return flag.astype(jnp.int32).astype(F32)

    zero = jnp.zeros((B, B), F32)

    def run_sums(keys, products, runs, count):
        total = zero
        for i in range(count):
            key = keys[i]
            before = keys[max(i - 1, 0)]
            total = as_mask(lax.div(before, 32) == lax.div(key, 32)) * total + products[lax.rem(key, 32)]
            runs[i] = total
        runs[count] = zero

    def orient(t, j, k):
        ahead = rp[0, t] == j
        small = jnp.where(ahead, j, 16 - j)
        large = jnp.where(ahead, 15 + k, 32 - k)
        return jnp.where(ahead, 0, 1), small, large, as_mask(ahead)

    def far_to_small(i, carry):
        for u in range(3):
            j = 3 * i + u + 1
            first, second = zero, zero
            for k in range(2, 9):
                turn, _, large, mask = orient(16 * k - j, j, k)
                value = product(16 * k - j, turn, large)
                first = first + mask * value
                second = second + (1.0 - mask) * value
            part[j] += first
            part[16 - j] += second
        return carry

    def far_to_large(k):
        first, second = zero, zero
        for j in range(1, 16):
            turn, small, _, mask = orient(16 * k - j, j, k)
            value = product(16 * k - j, 1 - turn, small)
            first = first + mask * value
            second = second + (1.0 - mask) * value
        for c, value in ((15 + k, first), (32 - k, second)):
            part[c] = value + wide_runs[wide_last[c]] + tight_runs[tight_last[c]]

    def far_pair(i, carry):
        far_to_large(2 * i + 1)
        far_to_large(2 * i + 2)
        return carry

    arrive(xs.at[pl.ds(17, 12)], block_recv)
    go(2, 2, xs.at[16 - 16 * par], xs.at[15 - 14 * par], cross_recv, partner)
    split_block(0, 0)
    lax.fori_loop(16, NC, split_block, 0, unroll=5)

    for m in range(1, 9):
        wide[m - 1] = product(16 * m, 0, rp[1, 16 * m])
        if m < 8:
            wide[m + 7] = product(16 * m, 1, rp[0, 16 * m])
    run_sums(wide_keys, wide, wide_runs, 15)

    def clear(c, carry):
        part[c] = zero
        return carry

    lax.fori_loop(0, 16, clear, 0)
    lax.fori_loop(0, 2, far_to_small, 0)
    for r, q in ((6, 7), (10, 8), (8, 6)):
        arrive(xs.at[r], g_recv.at[q])
        cross(r)
    lax.fori_loop(2, 5, far_to_small, 0)
    arrive(xs.at[pl.ds(1, 8)], cross_recv)
    lax.fori_loop(1, 16, split_block, 0, unroll=5)

    for t in range(16):
        tight[t] = product(t, 0, rp[1, t])
        if t > 0:
            tight[t + 15] = product(t, 1, rp[0, t])
    run_sums(tight_keys, tight, tight_runs, 31)

    def finish_small(c, carry):
        part[c] += wide_runs[wide_last[c]] + tight_runs[tight_last[c]]
        return carry

    lax.fori_loop(0, 16, finish_small, 0)
    part[16] = wide_runs[wide_last[16]] + tight_runs[tight_last[16]]

    for i in (3, 4, 2, 5, 1, 6, 0, 7):
        go(4, 2, part.at[2 * i + 1], cross_in.at[i], back_recv.at[i], partner)

    def fold_rows(value):
        total = value[0:8]
        for q in range(1, B // 8):
            total = total + value[8 * q : 8 * q + 8]
        return total

    def add_inner(c, carry):
        return carry + fold_rows(xs[c] * part[c])

    inner = lax.fori_loop(0, 17, add_inner, jnp.zeros((8, B), F32))
    far_to_large(2)

    def merge(c):
        i = c // 2 - 1 + par
        arrive(cross_in.at[i], back_recv.at[i])
        part[c] += cross_in[i]

    def send_relay(c, h, device, q):
        go(5, 1, part.at[c, half[h]], relay_in.at[3 * h + q], relay_recv.at[h], device)

    def send_near(c, h, q):
        go(5, 1, part.at[c, half[h]], near_in.at[2 * q + h], end_recv.at[0], near(c))

    for c in (8, 6, 10):
        merge(c)
    for h in (0, 1):
        send_relay(8, h, near(4), 0)
        send_relay(10, h, near(-2), 2)
        send_relay(6, h, near(2), 1)
    for c in (2, 14, 4, 12):
        merge(c)
    last = 16 - 16 * par
    i = 7 - 7 * par
    arrive(cross_in.at[i], back_recv.at[i])
    part[last] += cross_in[i]
    for c, q in ((14, 1), (2, 0)):
        for h in (0, 1):
            send_near(c, h, q)
    lax.fori_loop(1, 4, far_pair, 0)

    for e in (1, 3, 2):
        for d in (2, 1, 3):
            q = 3 * (e - 1) + d - 1
            go(6, 1, part.at[slot(e, d, 0, 0), low_half], half_a.at[q], half_recv.at[e - 1], at_y(d))
            go(6, 1, part.at[slot(d, e, 0, 0), high_half], half_b.at[q], half_recv.at[e + 2], at_x(d))

    inner = lax.fori_loop(17, NC, add_inner, inner)
    own = x_ref[...]
    norm = jnp.sum(fold_rows(own * own), axis=0, keepdims=True)
    inner = jnp.sum(inner, axis=0, keepdims=True)
    row_ids = lax.broadcasted_iota(jnp.int32, (8, B), 0)
    v_out[...] = jnp.where(row_ids == 0, inner, jnp.where(row_ids == 1, norm, 0.0))
    for k in range(1, 16):
        remote(v_out, v_near.at[k - 1], sent.at[8], sum_recv.at[0], near(k)).start()

    def send_axis(c, h, q, device):
        go(7, 1, part.at[c, half[h]], axis_in.at[q], end_recv.at[1], device)

    for e in (1, 3, 2):
        send_axis(slot(e, 0, 0, 0), 1, 5 + e, at_x(e))
        send_axis(slot(0, e, 0, 0), 0, 8 + e, at_y(e))

    for h in (0, 1):
        arrive(relay_in.at[pl.ds(3 * h, 3)], relay_recv.at[h])
        part[4, half[h]] += relay_in[3 * h] + relay_in[3 * h + 1]
        part[12, half[h]] += relay_in[3 * h + 2]
        send_near(4, h, 2)
        send_near(12, h, 3)

    arrive(v_near, sum_recv.at[0])
    mid = v_out[...]
    for k in range(15):
        mid = mid + v_near[k]
    v_mid[...] = mid
    for k in range(1, 16):
        remote(v_mid, v_far.at[k - 1], sent.at[9], sum_recv.at[1], near(16 * k)).start()

    for e in (1, 3, 2):
        at = slot(e, 0, 0, 0)
        q = 3 * (e - 1)
        arrive(half_a.at[pl.ds(q, 3)], half_recv.at[e - 1])
        part[at, low_half] += half_a[q] + half_a[q + 1] + half_a[q + 2]
        send_axis(at, 0, e - 1, at_x(e))
        at = slot(0, e, 0, 0)
        arrive(half_b.at[pl.ds(q, 3)], half_recv.at[e + 2])
        part[at, high_half] += half_b[q] + half_b[q + 1] + half_b[q + 2]
        send_axis(at, 1, 2 + e, at_y(e))

    arrive(near_in, end_recv.at[0])
    arrive(axis_in, end_recv.at[1])
    low = part[0, 0:HALF]
    high = part[0, HALF:B]
    for q in range(4):
        low = low + near_in[2 * q]
        high = high + near_in[2 * q + 1]
    for q in range(3):
        low = low + axis_in[q] + axis_in[9 + q]
        high = high + axis_in[3 + q] + axis_in[6 + q]
    image_ref[0:HALF] = low
    image_ref[HALF:B] = high
    arrive(v_far, sum_recv.at[1])
    total = v_mid[...]
    for k in range(15):
        total = total + v_far[k]
    step_ref[...] = jnp.broadcast_to(total[1:2] / total[0:1], (8, B))
    for group, count in enumerate(halves_sent):
        whole = tf.at[pl.ds(0, count // 2)]
        remote(whole, whole, sent.at[group], block_recv, partner).wait_send()
    remote(v_near, v_near, sent.at[8], block_recv, partner).wait_send()
    remote(v_near, v_near, sent.at[9], block_recv, partner).wait_send()


def update_kernel(x_ref, image_ref, step_ref, sol_ref, res_ref):
    own = x_ref[...]
    step = step_ref[0:1]
    sol_ref[...] = step * own
    res_ref[...] = own - step * image_ref[...]


def per_device(right_side, kernel_tiles, route_pairs):
    vmem = pltpu.VMEM
    dma = pltpu.SemaphoreType.DMA
    sems = [dma((10,)), dma((9,)), dma((6,)), dma(()), dma(()), dma((8,)), dma((2,)), dma((6,)), dma((2,)), dma((2,))]
    block = jax.ShapeDtypeStruct((B, B), F32)
    whole = pl.BlockSpec(memory_space=vmem)
    image, step = pl.pallas_call(
        cg_kernel,
        out_shape=(block, jax.ShapeDtypeStruct((8, B), F32)),
        in_specs=[pl.BlockSpec(memory_space=pltpu.SMEM), whole, pl.BlockSpec(memory_space=pl.ANY)],
        out_specs=(whole, whole),
        scratch_shapes=[
            vmem((NT, B, B), F32),
            vmem((NT, 2, B, 2 * B), BF16),
            vmem((NC, B, B), F32),
            vmem((NC, 2 * B, 2 * B), BF16),
            vmem((NC, B, B), F32),
            vmem((16, B, B), F32),
            vmem((31, B, B), F32),
            vmem((16, B, B), F32),
            vmem((32, B, B), F32),
            vmem((8, B, B), F32),
            vmem((6, HALF, B), F32),
            vmem((8, HALF, B), F32),
            vmem((12, HALF, B), F32),
            vmem((9, HALF, B), F32),
            vmem((9, HALF, B), F32),
            vmem((8, B), F32),
            vmem((8, B), F32),
            vmem((15, 8, B), F32),
            vmem((15, 8, B), F32),
            pltpu.SMEM((16,), jnp.int32),
            pltpu.SMEM((32,), jnp.int32),
            pltpu.SMEM((NC,), jnp.int32),
            pltpu.SMEM((NC,), jnp.int32),
            dma((CHUNKS,)),
        ]
        + sems,
        compiler_params=pltpu.CompilerParams(
            collective_id=0, has_side_effects=True, vmem_limit_bytes=60 * 1024 * 1024
        ),
    )(route_pairs.T, right_side, kernel_tiles)
    return pl.pallas_call(
        update_kernel,
        out_shape=(block, block),
        in_specs=[whole, whole, whole],
        out_specs=(whole, whole),
    )(right_side, image, step)


def solution(mesh):
    return jax.shard_map(
        per_device,
        mesh=mesh,
        in_specs=(P("blk", None), P("blk", None, None, None), P()),
        out_specs=(P("blk", None), P("blk", None)),
        check_vma=False,
    )
```

time: 547 us -> 58.5 us (0.11); the launches traced: 538 us -> 58.3 us
  starting transfers between devices: 257 us -> 0 us
  waiting for transfers between devices: 120 us -> 0 us
  blocking collectives: 74.3 us -> 0 us
  Pallas kernels: 0 us -> 57.7 us
  matrix products: 53.2 us -> 0 us
  local copies, waits for them, and re-layouts: 29.8 us -> 0 us
    ppermute x60 -> x0, starting transfers between devices: 257 us -> none  [shifted(): return lax.ppermute(value, axis, pairs)]
    ppermute x60 -> x0, waiting for transfers between devices: 120 us -> none  [shifted(): return lax.ppermute(value, axis, pairs)]
    psum x1 -> x0, blocking collectives: 74.3 us -> none  [column_total(): return lax.psum(jnp.sum(values, axis=0), 'blk')]
    pallas_call x0 -> x2, Pallas kernels: none -> 57.7 us  [the longest x1 56.2 us: per_device(): pl.pallas_call(cg_kernel, out_shape=(block, jax.ShapeDtypeStruct((8, B),...]
    dot_general x4 -> x0, matrix products: 53.2 us -> none  [the longest x1 20.1 us: per_device(): jnp.einsum('tij,tjr->tir', own_tiles, jnp.take(blocks, route_pairs[:, 1],...]
    dot_general x2 -> x0, local copies, waits for them, and re-layouts: 19 us -> none  [the longest x1 9.53 us: per_device(): jnp.einsum('tij,tjr->tir', own_tiles, jnp.take(blocks, route_pairs[:, 1],...]
    gather x2 -> x0, local copies, waits for them, and re-layouts: 8.86 us -> none  [the longest x1 4.43 us: per_device(): jnp.take(blocks, route_pairs[:, 1], axis=0)]
  transfers between devices with their start and end apart: 60 -> 0, of which waited for: 34 -> 0; matrix products, arithmetic and copies ran while one was open for 0% -> 0% of each run, Pallas kernels for 0% -> 0%
where the time goes in v2:
time: 58.5 us; the launch traced here: 58.3 us
  Pallas kernels  57.7 us (99%)
  between operations  0.64 us (1%)
    pallas_call x1, Pallas kernels, per_device(): pl.pallas_call(cg_kernel, out_shape=(block, jax.ShapeDtypeStruct((8, B),...  56.2 us
    pallas_call x1, Pallas kernels, per_device(): pl.pallas_call(update_kernel, out_shape=(block, block), in_specs=[whole,...  1.53 us

profile of v2, /device:TPU:1, one launch (start us, length us, event | category | flops | bytes accessed | tf_op | source)
XLA Modules:
  0.0 58.3 jit_solution(7711967749165035244)
XLA Ops:
  0.6 56.2 %shard_map.50 = (f32[128,128]{1,0:T(8,128)}, f32[8,128]{1,0:T(8,128)}) custom-call(s32[2,129]{1,0:T(2,128)} %bitcast.1, f32[128,128]{1,0:T(8,128)} %x_ref.3, f32[1,129,128,128]{3,2,1,0:T(8,128)} %tiles.1), custom_call_target="tpu_custom_call" | custom-call | tf_op jit(solution)/shard_map/pallas_call | solution.py:424
  56.8 1.5 %shard_map.51 = (f32[128,128]{1,0:T(8,128)}, f32[128,128]{1,0:T(8,128)}) custom-call(f32[128,128]{1,0:T(8,128)} %x_ref.3, f32[128,128]{1,0:T(8,128)} %get-tuple-element.4.image_ref, f32[8,128]{1,0:T(8,128)} %get-tuple-element.5.step_ref), custom_call_target="tpu_custom_call" | custom-call | tf_op jit(solution)/shard_map/pallas_call | solution.py:460

commit v3 on v2

v3 whole, which is shorter than its diff:
```python
import functools

import jax
import jax.numpy as jnp
from jax import lax
from jax.experimental import pallas as pl
from jax.experimental.pallas import tpu as pltpu
from jax.sharding import PartitionSpec as P

MESH = pl.DeviceIdType.MESH
NB = 256
B = 128
NT = 129
NC = 31
CHUNK = 16
CHUNKS = 9
HALF = B // 2
X_FIRST = 64
F32 = jnp.float32
BF16 = jnp.bfloat16


def split_pair(value):
    high = value.astype(BF16)
    low = (value - high.astype(F32)).astype(BF16)
    return high, low


def sort_network(count):
    pairs = []
    p = 1
    while p < count:
        k = p
        while k >= 1:
            for j in range(k % p, count - k, 2 * k):
                for i in range(min(k, count - j - k)):
                    if (i + j) // (2 * p) == (i + j + k) // (2 * p):
                        pairs.append((i + j, i + j + k))
            k //= 2
        p *= 2
    return pairs


def cg_kernel(
    rp, x_ref, tiles, image_ref, step_ref,
    tf, tb, xs, wb, part, wide, tight, wide_runs, tight_runs,
    cross_in, relay_in, near_in, axis_low, axis_high, half_a, half_b,
    v_out, v_mid, v_near, v_far, wide_keys, tight_keys, wide_last, tight_last,
    tile_sem, sent, g_recv, first_recv, early_recv, block_recv, cross_recv, back_recv, relay_recv, half_recv, end_recv, sum_recv,
):
    me = lax.axis_index("blk")
    par = lax.rem(me, 2)
    partner = me + 1 - 2 * par
    col = me // 16
    px = me // 64
    py = lax.rem(col, 4)

    def near(step):
        return lax.rem(me + step + NB, NB)

    def at_x(step):
        return me + (lax.rem(px + step, 4) - px) * 64

    def at_y(step):
        return me + (lax.rem(py + step, 4) - py) * 16

    def slot(dx, dy, tx, ty):
        owner_col = lax.rem(px + dx, 4) * 4 + lax.rem(py + dy, 4)
        there_col = lax.rem(px + tx, 4) * 4 + lax.rem(py + ty, 4)
        return 15 + lax.rem(owner_col - there_col + 16, 16)

    def remote(src, dst, send_sem, recv_sem, device):
        return pltpu.make_async_remote_copy(
            src_ref=src, dst_ref=dst, send_sem=send_sem, recv_sem=recv_sem,
            device_id=(device,), device_id_type=MESH,
        )

    def arrive(dst, recv_sem):
        remote(dst, dst, sent.at[0], recv_sem, partner).wait_recv()

    half = [pl.ds(0, HALF), pl.ds(HALF, HALF)]
    x_rows, y_rows = pl.ds(0, X_FIRST), pl.ds(X_FIRST, B - X_FIRST)
    rows_sent = [0] * 8

    def go(group, rows, src, dst, recv_sem, device):
        rows_sent[group] += rows
        remote(src, dst, sent.at[group], recv_sem, device).start()

    def tile_copy(q, count):
        span = pl.ds(q * CHUNK, count)
        return pltpu.make_async_copy(tiles.at[0, span], tf.at[span], tile_sem.at[q])


    barrier = pltpu.get_barrier_semaphore()
    axis_devices = [at_x(d) for d in (1, 2, 3)] + [at_y(d) for d in (1, 2, 3)]
    for device in axis_devices + [near(2), near(4), near(12), near(14), near(-2), near(-4), partner]:
        pl.semaphore_signal(barrier, inc=1, device_id=(device,), device_id_type=MESH)
    pl.semaphore_wait(barrier, 13)

    def own_to_x(d, rows, sem):
        go(0, rows.size, x_ref.at[rows], xs.at[slot(0, 0, d, 0), rows], sem, at_x(d))

    def own_to_y(d, rows, sem):
        go(0, rows.size, x_ref.at[rows], xs.at[slot(0, 0, 0, d), rows], sem, at_y(d))

    for h in (0, 1):
        go(1, HALF, x_ref.at[half[1 - h]], xs.at[12, half[1 - h]], g_recv.at[3 - h], near(-12))
        go(1, HALF, x_ref.at[half[h]], xs.at[4, half[h]], g_recv.at[h], near(-4))
    for d in (2, 1, 3):
        own_to_x(d, x_rows, first_recv.at[d - 1])
        own_to_y(d, y_rows, first_recv.at[2 + d])
    go(1, B, x_ref, xs.at[2], g_recv.at[4], near(-2))
    go(1, B, x_ref, xs.at[14], g_recv.at[5], near(-14))
    xs[0] = x_ref[...]
    for q in range(CHUNKS - 1):
        tile_copy(q, CHUNK).start()
    tile_copy(CHUNKS - 1, 1).start()

    def ordered(keys, count):
        keys = list(keys)
        for lower, upper in sort_network(count):
            if upper < len(keys):
                small, big = jnp.minimum(keys[lower], keys[upper]), jnp.maximum(keys[lower], keys[upper])
                keys[lower], keys[upper] = small, big
        return keys

    keys = [rp[0, 16 * m] * 32 + m - 1 for m in range(1, 9)]
    keys += [rp[1, 16 * m] * 32 + m + 7 for m in range(1, 8)]
    for i, key in enumerate(ordered(keys, 16)):
        wide_keys[i] = key
    keys = [rp[0, t] * 32 + t for t in range(16)] + [rp[1, t] * 32 + t + 15 for t in range(1, 16)]
    for i, key in enumerate(ordered(keys, 32)):
        tight_keys[i] = key

    def find_last(c, carry):
        for keys, last, count in ((wide_keys, wide_last, 15), (tight_keys, tight_last, 31)):
            found = jnp.int32(-1)
            for i in range(count):
                found = found + (keys[i] < (c + 1) * 32).astype(jnp.int32)
            ends_here = lax.div(keys[jnp.maximum(found, 0)], 32) == c
            last[c] = jnp.where(ends_here, found, count)
        return carry

    lax.fori_loop(0, NC, find_last, 0)


    def split_tile(t):
        high, low = split_pair(tf[t])
        tb[t, 0, :, 0:B] = high
        tb[t, 0, :, B : 2 * B] = low
        tb[t, 1, :, 0:B] = high.T
        tb[t, 1, :, B : 2 * B] = low.T

    def prepare(q, carry):
        tile_copy(q, CHUNK).wait()
        for u in range(CHUNK):
            split_tile(q * CHUNK + u)
        return carry

    def cross(r):
        go(2, B, xs.at[r], xs.at[r - 1 + 2 * par], cross_recv, partner)

    def forward(e):
        src = slot(e, 0, 0, 0)
        arrive(xs.at[src, x_rows], first_recv.at[3 - e])
        for d in (2, 1, 3):
            sem = early_recv if (e, d) == (1, 3) else block_recv
            go(3, X_FIRST, xs.at[src, x_rows], xs.at[slot(e, 0, 0, d), x_rows], sem, at_y(d))
        src = slot(0, e, 0, 0)
        arrive(xs.at[src, y_rows], first_recv.at[6 - e])
        for d in (2, 1, 3):
            sem = early_recv if (e, d) == (1, 3) else block_recv
            go(3, B - X_FIRST, xs.at[src, y_rows], xs.at[slot(0, e, d, 0), y_rows], sem, at_x(d))

    def forward_4(h):
        arrive(xs.at[4, half[h]], g_recv.at[h])
        if h == 0:
            go(1, HALF, xs.at[4, half[0]], xs.at[8, half[0]], g_recv.at[6], near(-4))
        go(1, HALF, xs.at[4, half[h]], xs.at[6, half[h]], g_recv.at[7], near(-2))

    def forward_12(h):
        arrive(xs.at[12, half[h]], g_recv.at[2 + h])
        if h == 1:
            go(1, HALF, xs.at[12, half[1]], xs.at[8, half[1]], g_recv.at[9], near(4))
        go(1, HALF, xs.at[12, half[h]], xs.at[10, half[h]], g_recv.at[8], near(2))

    forward(3)
    forward_4(0)
    forward(1)
    forward_4(1)
    forward_12(1)
    forward_12(0)
    for d in (3, 1, 2):
        own_to_y(d, x_rows, early_recv if d == 3 else block_recv)
        own_to_x(d, y_rows, block_recv)
    lax.fori_loop(0, 3, prepare, 0)
    forward(2)
    lax.fori_loop(3, CHUNKS - 1, prepare, 0)
    tile_copy(CHUNKS - 1, 1).wait()
    split_tile(NT - 1)
    for r in (4, 12):
        cross(r)
    for r, q in ((2, 4), (14, 5)):
        arrive(xs.at[r], g_recv.at[q])
        cross(r)

    def split_block(c, carry):
        high, low = split_pair(xs[c])
        wb[c, 0:B, 0:B] = high
        wb[c, 0:B, B : 2 * B] = low
        wb[c, B : 2 * B, 0:B] = high
        wb[c, B : 2 * B, B : 2 * B] = low
        return carry

    def product(t, turn, c):
        both = jnp.dot(tb[t, turn], wb[c], preferred_element_type=F32)
        return both[:, 0:B] + both[:, B : 2 * B]

    def as_mask(flag):
        return flag.astype(jnp.int32).astype(F32)

    zero = jnp.zeros((B, B), F32)

    def run_sums(keys, products, runs, count):
        total = zero
        for i in range(count):
            key = keys[i]
            before = keys[max(i - 1, 0)]
            total = as_mask(lax.div(before, 32) == lax.div(key, 32)) * total + products[lax.rem(key, 32)]
            runs[i] = total
        runs[count] = zero

    def orient(t, j, k):
        ahead = rp[0, t] == j
        small = jnp.where(ahead, j, 16 - j)
        large = jnp.where(ahead, 15 + k, 32 - k)
        return jnp.where(ahead, 0, 1), small, large, as_mask(ahead)

    def one_to_small(j):
        first, second = zero, zero
        for k in range(2, 9):
            turn, _, large, mask = orient(16 * k - j, j, k)
            value = product(16 * k - j, turn, large)
            first = first + mask * value
            second = second + (1.0 - mask) * value
        return first, second

    def far_to_small(j):
        first, second = one_to_small(j)
        third, fourth = one_to_small(16 - j)
        part[j] = first + fourth
        part[16 - j] = second + third

    def small_pair(i, carry):
        far_to_small(2 * i + 1)
        far_to_small(2 * i + 2)
        return carry

    def far_to_large(k):
        first, second = zero, zero
        for j in range(1, 16):
            turn, small, _, mask = orient(16 * k - j, j, k)
            value = product(16 * k - j, 1 - turn, small)
            first = first + mask * value
            second = second + (1.0 - mask) * value
        part[15 + k] = first
        part[32 - k] = second

    def large_pair(i, carry):
        far_to_large(2 * i + 1)
        far_to_large(2 * i + 2)
        return carry

    def add_runs(c, carry):
        part[c] += wide_runs[wide_last[c]] + tight_runs[tight_last[c]]
        return carry

    arrive(xs.at[pl.ds(0, 12), pl.ds(0, 16)], early_recv)
    go(2, B, xs.at[16 - 16 * par], xs.at[15 - 14 * par], cross_recv, partner)
    arrive(xs.at[pl.ds(0, 21), y_rows], block_recv)
    split_block(0, 0)
    lax.fori_loop(16, NC, split_block, 0, unroll=5)
    for m in range(1, 9):
        wide[m - 1] = product(16 * m, 0, rp[1, 16 * m])
        if m < 8:
            wide[m + 7] = product(16 * m, 1, rp[0, 16 * m])
    run_sums(wide_keys, wide, wide_runs, 15)
    for r, q in ((6, 7), (10, 8)):
        arrive(xs.at[r], g_recv.at[q])
        cross(r)
    lax.fori_loop(0, 2, small_pair, 0)
    arrive(xs.at[8, half[0]], g_recv.at[6])
    arrive(xs.at[8, half[1]], g_recv.at[9])
    cross(8)
    lax.fori_loop(2, 3, small_pair, 0)
    far_to_small(7)
    first, second = one_to_small(8)
    part[8] = first + second

    arrive(xs.at[pl.ds(1, 8)], cross_recv)
    lax.fori_loop(1, 16, split_block, 0, unroll=5)
    for t in range(16):
        tight[t] = product(t, 0, rp[1, t])
        if t > 0:
            tight[t + 15] = product(t, 1, rp[0, t])
    run_sums(tight_keys, tight, tight_runs, 31)

    def cross_back(i):
        go(4, B, part.at[2 * i + 1], cross_in.at[i], back_recv.at[i], partner)

    def finish_small(c, carry):
        part[c] += tight_runs[tight_last[c]]
        return carry

    lax.fori_loop(1, 16, finish_small, 0, unroll=5)
    for i in (3, 4, 2, 5, 1, 6, 0, 7):
        cross_back(i)
    part[0] = wide_runs[wide_last[0]] + tight_runs[tight_last[0]]
    part[16] = wide_runs[wide_last[16]] + tight_runs[tight_last[16]]

    def fold_rows(value):
        total = value[0:8]
        for q in range(1, B // 8):
            total = total + value[8 * q : 8 * q + 8]
        return total

    def add_inner(c, carry):
        return carry + fold_rows(xs[c] * part[c])

    inner = lax.fori_loop(0, 17, add_inner, jnp.zeros((8, B), F32), unroll=6)

    def merge(c):
        i = c // 2 - 1 + par
        arrive(cross_in.at[i], back_recv.at[i])
        part[c] += cross_in[i]

    def send_near(c, h, q):
        go(5, HALF, part.at[c, half[h]], near_in.at[2 * q + h], end_recv.at[0], near(c))

    far_to_large(2)
    for c in (8, 6, 10):
        merge(c)
    def send_relay(c, h, q, device):
        go(5, HALF, part.at[c, half[h]], relay_in.at[q], relay_recv.at[q // 3], device)

    send_relay(8, 0, 2, near(4))
    send_relay(8, 1, 5, near(-4))
    for h in (0, 1):
        send_relay(6, h, h, near(2))
        send_relay(10, h, 3 + h, near(-2))
    lax.fori_loop(1, 4, large_pair, 0)
    lax.fori_loop(17, NC, add_runs, 0, unroll=7)
    inner = lax.fori_loop(17, NC, add_inner, inner, unroll=7)
    own = x_ref[...]
    norm = jnp.sum(fold_rows(own * own), axis=0, keepdims=True)
    inner = jnp.sum(inner, axis=0, keepdims=True)
    row_ids = lax.broadcasted_iota(jnp.int32, (8, B), 0)
    v_out[...] = jnp.where(row_ids == 0, inner, jnp.where(row_ids == 1, norm, 0.0))
    for k in range(15, 0, -1):
        remote(v_out, v_near.at[k - 1], sent.at[8], sum_recv.at[0], near(k)).start()
    last = 16 - 16 * par
    i = 7 - 7 * par
    arrive(cross_in.at[i], back_recv.at[i])
    part[last] += cross_in[i]
    for e in (1, 3, 2):
        for d in (2, 1, 3):
            q = 3 * (e - 1) + d - 1
            go(6, X_FIRST, part.at[slot(e, d, 0, 0), x_rows], half_a.at[q], half_recv.at[e - 1], at_y(d))
            go(6, B - X_FIRST, part.at[slot(d, e, 0, 0), y_rows], half_b.at[q], half_recv.at[e + 2], at_x(d))
    for c in (14, 2, 12, 4):
        merge(c)
    for c, q in ((14, 1), (2, 0)):
        for h in (0, 1):
            send_near(c, h, q)

    def send_axis(c, rows, dst, device):
        go(7, rows.size, part.at[c, rows], dst, end_recv.at[1], device)

    for e in (1, 3, 2):
        send_axis(slot(e, 0, 0, 0), y_rows, axis_high.at[2 + e], at_x(e))
        send_axis(slot(0, e, 0, 0), x_rows, axis_low.at[2 + e], at_y(e))

    arrive(relay_in.at[pl.ds(0, 3)], relay_recv.at[0])
    part[4, half[0]] += relay_in[0] + relay_in[2]
    part[4, half[1]] += relay_in[1]
    for h in (0, 1):
        send_near(4, h, 2)
    arrive(relay_in.at[pl.ds(3, 3)], relay_recv.at[1])
    part[12, half[0]] += relay_in[3]
    part[12, half[1]] += relay_in[4] + relay_in[5]
    for h in (0, 1):
        send_near(12, h, 3)

    arrive(v_near, sum_recv.at[0])
    mid = v_out[...]
    for k in range(15):
        mid = mid + v_near[k]
    v_mid[...] = mid
    for k in range(1, 16):
        remote(v_mid, v_far.at[k - 1], sent.at[9], sum_recv.at[1], near(16 * k)).start()

    for e in (1, 3, 2):
        at = slot(e, 0, 0, 0)
        q = 3 * (e - 1)
        arrive(half_a.at[pl.ds(q, 3)], half_recv.at[e - 1])
        part[at, x_rows] += half_a[q] + half_a[q + 1] + half_a[q + 2]
        send_axis(at, x_rows, axis_low.at[e - 1], at_x(e))
        at = slot(0, e, 0, 0)
        arrive(half_b.at[pl.ds(q, 3)], half_recv.at[e + 2])
        part[at, y_rows] += half_b[q] + half_b[q + 1] + half_b[q + 2]
        send_axis(at, y_rows, axis_high.at[e - 1], at_y(e))

    arrive(near_in, end_recv.at[0])
    arrive(xs.at[pl.ds(0, 6)], end_recv.at[1])
    low = part[0, 0:HALF]
    high = part[0, HALF:B]
    for q in range(4):
        low = low + near_in[2 * q]
        high = high + near_in[2 * q + 1]
    image_ref[0:HALF] = low
    image_ref[HALF:B] = high
    low = image_ref[0:X_FIRST]
    high = image_ref[X_FIRST:B]
    for q in range(6):
        low = low + axis_low[q]
        high = high + axis_high[q]
    image_ref[0:X_FIRST] = low
    image_ref[X_FIRST:B] = high
    arrive(v_far, sum_recv.at[1])
    total = v_mid[...]
    for k in range(15):
        total = total + v_far[k]
    step_ref[...] = jnp.broadcast_to(total[1:2] / total[0:1], (8, B))
    for group, rows in enumerate(rows_sent):
        whole = tf.at[pl.ds(0, rows // B)]
        remote(whole, whole, sent.at[group], block_recv, partner).wait_send()
    remote(v_near, v_near, sent.at[8], block_recv, partner).wait_send()
    remote(v_near, v_near, sent.at[9], block_recv, partner).wait_send()


def update_kernel(x_ref, image_ref, step_ref, sol_ref, res_ref):
    own = x_ref[...]
    step = step_ref[0:1]
    sol_ref[...] = step * own
    res_ref[...] = own - step * image_ref[...]


def per_device(right_side, kernel_tiles, route_pairs):
    vmem = pltpu.VMEM
    dma = pltpu.SemaphoreType.DMA
    sems = [dma((10,)), dma((10,)), dma((6,)), dma(()), dma(()), dma(()), dma((8,)), dma((2,)), dma((6,)), dma((2,)), dma((2,))]
    block = jax.ShapeDtypeStruct((B, B), F32)
    whole = pl.BlockSpec(memory_space=vmem)
    image, step = pl.pallas_call(
        cg_kernel,
        out_shape=(block, jax.ShapeDtypeStruct((8, B), F32)),
        in_specs=[pl.BlockSpec(memory_space=pltpu.SMEM), whole, pl.BlockSpec(memory_space=pl.ANY)],
        out_specs=(whole, whole),
        scratch_shapes=[
            vmem((NT, B, B), F32),
            vmem((NT, 2, B, 2 * B), BF16),
            vmem((NC, B, B), F32),
            vmem((NC, 2 * B, 2 * B), BF16),
            vmem((NC, B, B), F32),
            vmem((16, B, B), F32),
            vmem((31, B, B), F32),
            vmem((16, B, B), F32),
            vmem((32, B, B), F32),
            vmem((8, B, B), F32),
            vmem((6, HALF, B), F32),
            vmem((8, HALF, B), F32),
            vmem((6, X_FIRST, B), F32),
            vmem((6, B - X_FIRST, B), F32),
            vmem((9, X_FIRST, B), F32),
            vmem((9, B - X_FIRST, B), F32),
            vmem((8, B), F32),
            vmem((8, B), F32),
            vmem((15, 8, B), F32),
            vmem((15, 8, B), F32),
            pltpu.SMEM((16,), jnp.int32),
            pltpu.SMEM((32,), jnp.int32),
            pltpu.SMEM((NC,), jnp.int32),
            pltpu.SMEM((NC,), jnp.int32),
            dma((CHUNKS,)),
        ]
        + sems,
        compiler_params=pltpu.CompilerParams(
            collective_id=0, has_side_effects=True, vmem_limit_bytes=60 * 1024 * 1024
        ),
    )(route_pairs.T, right_side, kernel_tiles)
    return pl.pallas_call(
        update_kernel,
        out_shape=(block, block),
        in_specs=[whole, whole, whole],
        out_specs=(whole, whole),
    )(right_side, image, step)


def solution(mesh):
    return jax.shard_map(
        per_device,
        mesh=mesh,
        in_specs=(P("blk", None), P("blk", None, None, None), P()),
        out_specs=(P("blk", None), P("blk", None)),
        check_vma=False,
    )
```

time: 58.5 us -> 56.4 us (0.964)
  Pallas kernels: 57.7 us -> 55.5 us
    pallas_call x1, Pallas kernels: 56.2 us -> 53.9 us  [per_device(): pl.pallas_call(cg_kernel, out_shape=(block, jax.ShapeDtypeStruct((8, B),...]
where the time goes in v3:
time: 56.4 us; the launch traced here: 56.1 us
  Pallas kernels  55.5 us (98%)
  between operations  0.64 us (1%)
    pallas_call x1, Pallas kernels, per_device(): pl.pallas_call(cg_kernel, out_shape=(block, jax.ShapeDtypeStruct((8, B),...  53.9 us
    pallas_call x1, Pallas kernels, per_device(): pl.pallas_call(update_kernel, out_shape=(block, block), in_specs=[whole,...  1.53 us

profile of v3, /device:TPU:1, one launch (start us, length us, event | category | flops | bytes accessed | tf_op | source)
XLA Modules:
  0.0 56.1 jit_solution(2001284762483108648)
XLA Ops:
  0.6 53.9 %shard_map.50 = (f32[128,128]{1,0:T(8,128)}, f32[8,128]{1,0:T(8,128)}) custom-call(s32[2,129]{1,0:T(2,128)} %bitcast.1, f32[128,128]{1,0:T(8,128)} %x_ref.3, f32[1,129,128,128]{3,2,1,0:T(8,128)} %tiles.1), custom_call_target="tpu_custom_call" | custom-call | tf_op jit(solution)/shard_map/pallas_call | solution.py:454
  54.6 1.5 %shard_map.51 = (f32[128,128]{1,0:T(8,128)}, f32[128,128]{1,0:T(8,128)}) custom-call(f32[128,128]{1,0:T(8,128)} %x_ref.3, f32[128,128]{1,0:T(8,128)} %get-tuple-element.4.image_ref, f32[8,128]{1,0:T(8,128)} %get-tuple-element.5.step_ref), custom_call_target="tpu_custom_call" | custom-call | tf_op jit(solution)/shard_map/pallas_call | solution.py:491

commit v4 on v3

--- a/solution.py
+++ b/solution.py
@@ -42,11 +42,12 @@
 
 
 def cg_kernel(
-    rp, x_ref, tiles, image_ref, step_ref,
+    pairs_hbm, x_hbm, tiles, image_ref, step_ref,
+    rp,
     tf, tb, xs, wb, part, wide, tight, wide_runs, tight_runs,
     cross_in, relay_in, near_in, axis_low, axis_high, half_a, half_b,
     v_out, v_mid, v_near, v_far, wide_keys, tight_keys, wide_last, tight_last,
-    tile_sem, sent, g_recv, first_recv, early_recv, block_recv, cross_recv, back_recv, relay_recv, half_recv, end_recv, sum_recv,
+    tile_sem, own_sem, pairs_sem, sent, g_recv, first_recv, early_recv, block_recv, cross_recv, back_recv, relay_recv, half_recv, end_recv, sum_recv,
 ):
     me = lax.axis_index("blk")
     par = lax.rem(me, 2)
@@ -86,6 +87,11 @@
         rows_sent[group] += rows
         remote(src, dst, sent.at[group], recv_sem, device).start()
 
+    own_copy = pltpu.make_async_copy(x_hbm, xs.at[0], own_sem)
+    own_copy.start()
+    pairs_copy = pltpu.make_async_copy(pairs_hbm, rp, pairs_sem)
+    pairs_copy.start()
+
     def tile_copy(q, count):
         span = pl.ds(q * CHUNK, count)
         return pltpu.make_async_copy(tiles.at[0, span], tf.at[span], tile_sem.at[q])
@@ -95,23 +101,23 @@
     axis_devices = [at_x(d) for d in (1, 2, 3)] + [at_y(d) for d in (1, 2, 3)]
     for device in axis_devices + [near(2), near(4), near(12), near(14), near(-2), near(-4), partner]:
         pl.semaphore_signal(barrier, inc=1, device_id=(device,), device_id_type=MESH)
+    own_copy.wait()
     pl.semaphore_wait(barrier, 13)
 
     def own_to_x(d, rows, sem):
-        go(0, rows.size, x_ref.at[rows], xs.at[slot(0, 0, d, 0), rows], sem, at_x(d))
+        go(0, rows.size, xs.at[0, rows], xs.at[slot(0, 0, d, 0), rows], sem, at_x(d))
 
     def own_to_y(d, rows, sem):
-        go(0, rows.size, x_ref.at[rows], xs.at[slot(0, 0, 0, d), rows], sem, at_y(d))
+        go(0, rows.size, xs.at[0, rows], xs.at[slot(0, 0, 0, d), rows], sem, at_y(d))
 
     for h in (0, 1):
-        go(1, HALF, x_ref.at[half[1 - h]], xs.at[12, half[1 - h]], g_recv.at[3 - h], near(-12))
-        go(1, HALF, x_ref.at[half[h]], xs.at[4, half[h]], g_recv.at[h], near(-4))
+        go(1, HALF, xs.at[0, half[1 - h]], xs.at[12, half[1 - h]], g_recv.at[3 - h], near(-12))
+        go(1, HALF, xs.at[0, half[h]], xs.at[4, half[h]], g_recv.at[h], near(-4))
     for d in (2, 1, 3):
         own_to_x(d, x_rows, first_recv.at[d - 1])
         own_to_y(d, y_rows, first_recv.at[2 + d])
-    go(1, B, x_ref, xs.at[2], g_recv.at[4], near(-2))
-    go(1, B, x_ref, xs.at[14], g_recv.at[5], near(-14))
-    xs[0] = x_ref[...]
+    go(1, B, xs.at[0], xs.at[2], g_recv.at[4], near(-2))
+    go(1, B, xs.at[0], xs.at[14], g_recv.at[5], near(-14))
     for q in range(CHUNKS - 1):
         tile_copy(q, CHUNK).start()
     tile_copy(CHUNKS - 1, 1).start()
@@ -124,6 +130,7 @@
                 keys[lower], keys[upper] = small, big
         return keys
 
+    pairs_copy.wait()
     keys = [rp[0, 16 * m] * 32 + m - 1 for m in range(1, 9)]
     keys += [rp[1, 16 * m] * 32 + m + 7 for m in range(1, 8)]
     for i, key in enumerate(ordered(keys, 16)):
@@ -351,7 +358,7 @@
     lax.fori_loop(1, 4, large_pair, 0)
     lax.fori_loop(17, NC, add_runs, 0, unroll=7)
     inner = lax.fori_loop(17, NC, add_inner, inner, unroll=7)
-    own = x_ref[...]
+    own = xs[0]
     norm = jnp.sum(fold_rows(own * own), axis=0, keepdims=True)
     inner = jnp.sum(inner, axis=0, keepdims=True)
     row_ids = lax.broadcasted_iota(jnp.int32, (8, B), 0)
@@ -380,16 +387,16 @@
         send_axis(slot(e, 0, 0, 0), y_rows, axis_high.at[2 + e], at_x(e))
         send_axis(slot(0, e, 0, 0), x_rows, axis_low.at[2 + e], at_y(e))
 
+    arrive(relay_in.at[pl.ds(3, 3)], relay_recv.at[1])
+    part[12, half[0]] += relay_in[3]
+    part[12, half[1]] += relay_in[4] + relay_in[5]
+    for h in (0, 1):
+        send_near(12, h, 3)
     arrive(relay_in.at[pl.ds(0, 3)], relay_recv.at[0])
     part[4, half[0]] += relay_in[0] + relay_in[2]
     part[4, half[1]] += relay_in[1]
     for h in (0, 1):
         send_near(4, h, 2)
-    arrive(relay_in.at[pl.ds(3, 3)], relay_recv.at[1])
-    part[12, half[0]] += relay_in[3]
-    part[12, half[1]] += relay_in[4] + relay_in[5]
-    for h in (0, 1):
-        send_near(12, h, 3)
 
     arrive(v_near, sum_recv.at[0])
     mid = v_out[...]
@@ -454,9 +461,10 @@
     image, step = pl.pallas_call(
         cg_kernel,
         out_shape=(block, jax.ShapeDtypeStruct((8, B), F32)),
-        in_specs=[pl.BlockSpec(memory_space=pltpu.SMEM), whole, pl.BlockSpec(memory_space=pl.ANY)],
+        in_specs=[pl.BlockSpec(memory_space=pl.ANY)] * 3,
         out_specs=(whole, whole),
         scratch_shapes=[
+            pltpu.SMEM((2, NT), jnp.int32),
             vmem((NT, B, B), F32),
             vmem((NT, 2, B, 2 * B), BF16),
             vmem((NC, B, B), F32),
@@ -482,6 +490,8 @@
             pltpu.SMEM((NC,), jnp.int32),
             pltpu.SMEM((NC,), jnp.int32),
             dma((CHUNKS,)),
+            dma(()),
+            dma(()),
         ]
         + sems,
         compiler_params=pltpu.CompilerParams(

time: 56.4 us -> 55.6 us (0.986)
  Pallas kernels: 55.5 us -> 54.6 us
    pallas_call x1, Pallas kernels: 53.9 us -> 53.1 us  [per_device(): pl.pallas_call(cg_kernel, out_shape=(block, jax.ShapeDtypeStruct((8, B),...]
where the time goes in v4:
time: 55.6 us; the launch traced here: 55.3 us
  Pallas kernels  54.6 us (98%)
  between operations  0.64 us (1%)
    pallas_call x1, Pallas kernels, per_device(): pl.pallas_call(cg_kernel, out_shape=(block, jax.ShapeDtypeStruct((8, B),...  53.1 us
    pallas_call x1, Pallas kernels, per_device(): pl.pallas_call(update_kernel, out_shape=(block, block), in_specs=[whole,...  1.53 us

profile of v4, /device:TPU:1, one launch (start us, length us, event | category | flops | bytes accessed | tf_op | source)
XLA Modules:
  0.0 55.3 jit_solution(9074599440280926147)
XLA Ops:
  0.6 53.1 %shard_map.50 = (f32[128,128]{1,0:T(8,128)}, f32[8,128]{1,0:T(8,128)}) custom-call(s32[2,129]{1,0:T(2,128)} %bitcast.1, f32[128,128]{1,0:T(8,128)} %x_ref.1, f32[1,129,128,128]{3,2,1,0:T(8,128)} %tiles.1), custom_call_target="tpu_custom_call" | custom-call | tf_op jit(solution)/shard_map/pallas_call | solution.py:461
  53.7 1.5 %shard_map.51 = (f32[128,128]{1,0:T(8,128)}, f32[128,128]{1,0:T(8,128)}) custom-call(f32[128,128]{1,0:T(8,128)} %x_ref.1, f32[128,128]{1,0:T(8,128)} %get-tuple-element.4.image_ref, f32[8,128]{1,0:T(8,128)} %get-tuple-element.5.step_ref), custom_call_target="tpu_custom_call" | custom-call | tf_op jit(solution)/shard_map/pallas_call | solution.py:501

commit v5 on v4

--- a/solution.py
+++ b/solution.py
@@ -282,6 +282,9 @@
         part[c] += wide_runs[wide_last[c]] + tight_runs[tight_last[c]]
         return carry
 
+    for r, q in ((6, 7), (10, 8)):
+        arrive(xs.at[r], g_recv.at[q])
+        cross(r)
     arrive(xs.at[pl.ds(0, 12), pl.ds(0, 16)], early_recv)
     go(2, B, xs.at[16 - 16 * par], xs.at[15 - 14 * par], cross_recv, partner)
     arrive(xs.at[pl.ds(0, 21), y_rows], block_recv)
@@ -292,13 +295,10 @@
         if m < 8:
             wide[m + 7] = product(16 * m, 1, rp[0, 16 * m])
     run_sums(wide_keys, wide, wide_runs, 15)
-    for r, q in ((6, 7), (10, 8)):
-        arrive(xs.at[r], g_recv.at[q])
-        cross(r)
-    lax.fori_loop(0, 2, small_pair, 0)
     arrive(xs.at[8, half[0]], g_recv.at[6])
     arrive(xs.at[8, half[1]], g_recv.at[9])
     cross(8)
+    lax.fori_loop(0, 2, small_pair, 0)
     lax.fori_loop(2, 3, small_pair, 0)
     far_to_small(7)
     first, second = one_to_small(8)

time: 55.6 us -> 57.3 us (1.031)
  Pallas kernels: 54.6 us -> 56.5 us
    pallas_call x1, Pallas kernels: 53.1 us -> 54.9 us  [per_device(): pl.pallas_call(cg_kernel, out_shape=(block, jax.ShapeDtypeStruct((8, B),...]
where the time goes in v5:
time: 57.3 us; the launch traced here: 57.1 us
  Pallas kernels  56.5 us (99%)
  between operations  0.64 us (1%)
    pallas_call x1, Pallas kernels, per_device(): pl.pallas_call(cg_kernel, out_shape=(block, jax.ShapeDtypeStruct((8, B),...  54.9 us
    pallas_call x1, Pallas kernels, per_device(): pl.pallas_call(update_kernel, out_shape=(block, block), in_specs=[whole,...  1.53 us

profile of v5, /device:TPU:1, one launch (start us, length us, event | category | flops | bytes accessed | tf_op | source)
XLA Modules:
  0.0 57.1 jit_solution(15552022585216986318)
XLA Ops:
  0.6 54.9 %shard_map.50 = (f32[128,128]{1,0:T(8,128)}, f32[8,128]{1,0:T(8,128)}) custom-call(s32[2,129]{1,0:T(2,128)} %bitcast.1, f32[128,128]{1,0:T(8,128)} %x_ref.1, f32[1,129,128,128]{3,2,1,0:T(8,128)} %tiles.1), custom_call_target="tpu_custom_call" | custom-call | tf_op jit(solution)/shard_map/pallas_call | solution.py:461
  55.6 1.5 %shard_map.51 = (f32[128,128]{1,0:T(8,128)}, f32[128,128]{1,0:T(8,128)}) custom-call(f32[128,128]{1,0:T(8,128)} %x_ref.1, f32[128,128]{1,0:T(8,128)} %get-tuple-element.4.image_ref, f32[8,128]{1,0:T(8,128)} %get-tuple-element.5.step_ref), custom_call_target="tpu_custom_call" | custom-call | tf_op jit(solution)/shard_map/pallas_call | solution.py:501
